TPU v7x, 128 devices: a whole 4x4x4 slice. The times are simulated.
128 devices in a mesh: mem: 32 (over y, z_hi, x), ty: 2 (over core), tx: 2 (over z_lo).
Axes of the slice: x: 4, y: 4, z: 4 (z_hi: 2, z_lo: 2; z = z_hi * 2 + z_lo), core: 2. Of those that a mesh axis runs over, the one named last changes fastest.
Arguments:
- predicted_states: float32 [512, 3, 64, 512], P('mem', None, 'ty', 'tx'), may hold values from -6 to 6
- undisturbed_thickness_ratio: float32 [64, 512], P('ty', 'tx'), may hold values from 0.5 to 1.5
- sampled_location: int32 [2, 2, 65536], P('ty', 'tx'), may hold values from 0 to 8191
- measured_height: float32 [2, 2, 65536], P('ty', 'tx', 'mem'), may hold values from -6 to 6
- gauge_uncertainty: float32 [2, 2, 65536], P('ty', 'tx', 'mem'), may hold values from 0.5 to 1.5
- gauge_tally: int32 [2, 2, 32], P('ty', 'tx', 'mem'), may hold values from 128 to 2048, as said below
Outputs:
- analysis: bfloat16 [512, 3, 64, 512], P('mem', None, 'ty', 'tx')
Inputs may be any that keep to these rules, and one draw needn't show every extreme that they name: `gauge_tally`: every entry is a multiple of 128; in every tile some region has exactly 2048 used slots; the used slots of a region come first. `sampled_location`: A flat index tile row * 256 + tile column within the slot's own tile.
All inputs are finite; a program needn't handle non-finite values.
Results may differ from a plain program's by a relative error of at most 0.012.
The roundings to bfloat16 on the way count: a program that leaves them out, or rounds other values in their place, can miss the bound.
Values may be sent and summed in bfloat16 or wider, within the bound.
No kernel may reach another device: no remote copies, remote signals or barrier semaphores. Data moves between devices by JAX's collectives and lax.ppermute only.
A program may use at most 128 MiB of HBM per device.

v0:
```python
import jax
import jax.numpy as jnp
from jax import lax
from jax.sharding import PartitionSpec as P

NSI = 12
STEPS = 2


HALF_NU = 0.35
ONE_THIRD = 1.0 / 3.0
TWO_THIRD = 2.0 / 3.0


def extended(array, sides, width):
    for axis, dim in sides:
        size, length = (lax.axis_size(axis), array.shape[dim])
        up = [(i, (i + 1) % size) for i in range(size)]
        down = [(j, i) for i, j in up]
        last = lax.slice_in_dim(array, length - width, length, axis=dim)
        initial = lax.slice_in_dim(array, 0, width, axis=dim)
        before = lax.ppermute(last, axis, up)
        after = lax.ppermute(initial, axis, down)
        array = jnp.concatenate([before, array, after], axis=dim)
    return array


def tendency(padded, depth_inner):
    height = padded[..., 0, :, :]
    zonal = padded[..., 1, :, :]
    meridional = padded[..., 2, :, :]
    divergence = (
        zonal[..., 1:-1, 2:]
        - zonal[..., 1:-1, :-2]
        + (meridional[..., 2:, 1:-1] - meridional[..., :-2, 1:-1])
    )
    height_rate = -HALF_NU * depth_inner * divergence
    zonal_rate = -HALF_NU * (height[..., 1:-1, 2:] - height[..., 1:-1, :-2])
    merid_rate = -HALF_NU * (height[..., 2:, 1:-1] - height[..., :-2, 1:-1])
    return jnp.stack([height_rate, zonal_rate, merid_rate], axis=-3)


def transform_weights(gathered, values, errors, total):
    members = gathered.shape[0]
    slots = gathered.shape[1]
    row_index = jnp.arange(slots, dtype=jnp.int32)
    row_mask = (row_index < total).astype(jnp.float32)
    obs_wide = gathered.astype(jnp.float32)
    obs_mean = jnp.mean(obs_wide, axis=0)
    weight_scale = row_mask / errors
    scaled_dev = ((obs_wide - obs_mean) * weight_scale).astype(jnp.bfloat16)
    scaled_innov = ((values - obs_mean) * weight_scale).astype(jnp.bfloat16)
    gram_matrix = jnp.dot(scaled_dev, scaled_dev.T, preferred_element_type=jnp.float32)
    identity_k = jnp.eye(members, dtype=jnp.float32)
    system = gram_matrix + (members - 1.0) * identity_k
    frob_norm = jnp.sqrt(jnp.sum(system * system))
    root_iter = (system / frob_norm).astype(jnp.bfloat16)
    inverse_root = identity_k.astype(jnp.bfloat16)
    for iteration in range(NSI):
        product = jnp.dot(inverse_root, root_iter, preferred_element_type=jnp.float32)
        correction = (1.5 * identity_k - 0.5 * product).astype(jnp.bfloat16)
        root_iter = jnp.dot(root_iter, correction, preferred_element_type=jnp.float32).astype(
            jnp.bfloat16
        )
        inverse_root = jnp.dot(correction, inverse_root, preferred_element_type=jnp.float32).astype(
            jnp.bfloat16
        )
    projected = jnp.dot(scaled_dev, scaled_innov, preferred_element_type=jnp.float32)
    inverse_wide = inverse_root.astype(jnp.float32)
    inner_step = jnp.dot(inverse_wide, projected, precision=lax.Precision.HIGHEST)
    mean_weights = jnp.dot(inverse_wide, inner_step, precision=lax.Precision.HIGHEST) / frob_norm
    weights = (jnp.sqrt((members - 1.0) / frob_norm) * inverse_wide + mean_weights[:, None]).astype(
        jnp.bfloat16
    )
    return weights


def apply_weights(weights, regrouped):
    members = regrouped.shape[0]
    flat = regrouped.reshape(members, -1)
    mean_field = jnp.mean(flat.astype(jnp.float32), axis=0)
    deviation = (flat.astype(jnp.float32) - mean_field).astype(jnp.bfloat16)
    mixed = jnp.dot(weights.T, deviation, preferred_element_type=jnp.float32)
    return (mean_field + mixed).astype(jnp.bfloat16).reshape(regrouped.shape)


def shards(
    predicted_states,
    undisturbed_thickness_ratio,
    sampled_location,
    measured_height,
    gauge_uncertainty,
    gauge_tally,
):
    trajectory_states = predicted_states

    def rimmed(current):
        return extended(current, (("ty", 2), ("tx", 3)), 1)

    for iteration in range(STEPS):
        first = trajectory_states + tendency(rimmed(trajectory_states), undisturbed_thickness_ratio)
        second = 0.75 * trajectory_states + 0.25 * (
            first + tendency(rimmed(first), undisturbed_thickness_ratio)
        )
        trajectory_states = ONE_THIRD * trajectory_states + TWO_THIRD * (
            second + tendency(rimmed(second), undisturbed_thickness_ratio)
        )
    background_trajectories = trajectory_states.astype(jnp.bfloat16)
    height_flat = background_trajectories[:, 0].reshape(background_trajectories.shape[0], -1)
    cell_index = sampled_location.reshape(-1)
    taken = jnp.take(height_flat, cell_index, axis=1)
    gathered = lax.all_to_all(taken, "mem", split_axis=1, concat_axis=0, tiled=True)
    weights = transform_weights(
        gathered,
        measured_height.reshape(-1),
        gauge_uncertainty.reshape(-1),
        gauge_tally.reshape(()),
    )
    updated = apply_weights(
        weights,
        lax.all_to_all(background_trajectories, "mem", split_axis=2, concat_axis=0, tiled=True),
    )
    return lax.all_to_all(updated, "mem", split_axis=0, concat_axis=2, tiled=True)


def solution(mesh):
    in_specs = (
        P("mem", None, "ty", "tx"),
        P("ty", "tx"),
        P("ty", "tx", None),
        P("ty", "tx", "mem"),
        P("ty", "tx", "mem"),
        P("ty", "tx", "mem"),
    )
    out_specs = P("mem", None, "ty", "tx")
    return jax.shard_map(shards, mesh=mesh, in_specs=in_specs, out_specs=out_specs, check_vma=False)
```

profile of v0, /device:TPU:0, one launch (start us, length us, event | category | flops | bytes accessed | tf_op | source)
XLA Modules:
  0.0 491.0 jit_solution(16502582433330413966)
XLA Ops:
  1.8 6.2 %copy.142 = f32[16,3,32,256]{2,0,3,1:T(8,128)} copy(f32[16,3,32,256]{3,2,1,0:T(8,128)} %param.6) | data formatting | bytes 3145728 | tf_op args[0]
  8.0 4.7 copy.141
  12.7 4.8 copy.143
  17.4 8.2 %pad_maximum_fusion = f32[16,3,34,256]{2,0,3,1:T(8,128)S(1)} fusion(f32[16,3,1,256]{2,0,3,1:T(8,128)} %copy.143, f32[16,3,32,256]{2,0,3,1:T(8,128)} %copy.142, f32[16,3,1,256]{2,0,3,1:T(8,128)} %copy.141), kind=kLoop, calls=%fused_computation.1 | loop fusion | flops 835584 | bytes 3342336 | tf_op jit(solution)/shard_map/concatenate | solution.py:24
  25.6 2.6 copy-done.1
  28.3 2.0 collective-permute-start.2
  30.4 5.7 %copy.145 = f32[16,3,34,256]{3,0,2,1:T(8,128)S(1)} copy(f32[16,3,34,256]{2,0,3,1:T(8,128)} %copy-done.1) | data formatting | bytes 3342336 | tf_op jit(solution)/shard_map/concatenate | solution.py:24
  42.3 1.5 fusion.86
  43.8 1.6 copy.176
  45.4 2.0 collective-permute-start.6
  47.4 1.6 copy.177
  50.7 2.4 collective-permute-done.7
  54.5 2.3 pad_maximum_fusion.2
  59.4 1.5 fusion.3
  62.5 1.5 fusion.85
  64.0 1.6 copy.178
  65.7 1.6 copy.179
  67.3 2.0 collective-permute-start.11
  72.6 2.3 pad_maximum_fusion.3
  77.3 1.4 fusion.5
  81.1 14.7 %collective-permute-start.14 = (f32[16,3,34,1]{2,0,3,1:T(8,128)S(1)}, f32[16,3,34,1]{2,0,3,1:T(8,128)S(1)}, u32[]{:S(2)}, u32[]{:S(2)}) collective-permute-start(f32[16,3,34,1]{2,0,3,1:T(8,128)S(1)} %copy.180), channel_id=1, source_target_pairs={{0,1},{1,0},{2,3},{3,2},{4,5},{5,4},{6,7},{7,6},{8,9},{9,8},{10,11... | collective-permute-start | bytes 19592 | tf_op jit(solution)/shard_map/ppermute | solution.py:22
  98.2 2.0 collective-permute-done.15
  105.1 1.5 fusion.83
  106.6 1.6 copy.182
  108.4 1.6 copy.183
  110.0 1.9 collective-permute-start.19
  115.3 2.3 pad_maximum_fusion.5
  122.6 1.5 fusion.82
  124.1 1.6 copy.184
  125.6 1.9 collective-permute-start.22
  127.6 1.6 copy.185
  129.4 1.7 broadcast_clamp_fusion
  131.7 3.0 reduce.9
  134.7 1.7 reshape.144
  137.7 1.4 copy.167
  139.1 2.3 pad_maximum_fusion.6
  146.5 10.7 %all-to-all-start = ((bf16[16,3,32,256]{3,0,1,2:T(8,128)(2,1)}), bf16[16,3,32,256]{3,0,1,2:T(8,128)(2,1)S(1)}, u32[]{:S(2)}, u32[]{:S(2)}) async-start(bf16[16,3,32,256]{3,0,1,2:T(8,128)(2,1)} %copy.168), calls=%async_computation | async-start | bytes 1572864 | tf_op jit(solution)/shard_map/all_to_all | solution.py:121
  158.3 229.0 %gather_fusion = bf16[65536,16]{1,0:T(8,128)(2,1)} fusion(bf16[16,8192]{0,1:T(8,128)(2,1)S(1)} %bitcast.183, s32[65536]{0:T(1024)S(1)} %copy-done.35), kind=kCustom, calls=%fused_computation | custom fusion | bytes 4456448 | tf_op jit(solution)/shard_map/jit(_take)/gather | solution.py:111
  387.3 12.8 %copy.170 = bf16[16,32,2048]{2,0,1:T(8,128)(2,1)S(1)} copy(bf16[16,32,2048]{0,2,1:T(8,128)(2,1)} %bitcast.184) | data formatting | bytes 4194304 | tf_op jit(solution)/shard_map/jit(_take)/gather | solution.py:111
  400.1 1.6 broadcast_select_fusion
  401.8 10.1 %all-to-all-start.1 = ((bf16[16,32,2048]{2,0,1:T(8,128)(2,1)}), bf16[16,32,2048]{2,0,1:T(8,128)(2,1)S(1)}, u32[]{:S(2)}, u32[]{:S(2)}) async-start(bf16[16,32,2048]{2,0,1:T(8,128)(2,1)} %broadcast_select_fusion), calls=%async_computation.1 | async-start | bytes 4194304 | tf_op jit(solution)/shard_map/all_to_all | solution.py:112
  414.1 1.5 copy.186
  415.7 24.7 %all-to-all-done.1 = bf16[16,32,2048]{2,0,1:T(8,128)(2,1)S(1)} async-done(((bf16[16,32,2048]{2,0,1:T(8,128)(2,1)}), bf16[16,32,2048]{2,0,1:T(8,128)(2,1)S(1)}, u32[]{:S(2)}, u32[]{:S(2)}) %all-to-all-start.1) | async-done | bytes 2097184 | tf_op jit(solution)/shard_map/all_to_all | solution.py:112
  441.5 2.0 multiply_reduce_fusion
  458.4 1.5 convolution_convert_fusion.2
  459.8 2.1 convolution_convert_fusion
  463.7 2.1 add_convert_fusion
  466.8 22.5 %all_to_all.37 = bf16[512,3,1,256]{3,1,2,0:T(4,128)(2,1)S(1)} all-to-all(bf16[512,3,1,256]{3,1,2,0:T(4,128)(2,1)S(1)} %copy.173), channel_id=1, replica_groups=mesh['mem'=32,'ty'=2,'tx'=2] {'mem'}, dimensions={0} | all-to-all | bytes 1572864 | tf_op jit(solution)/shard_map/all_to_all | solution.py:123
  (230 shorter events, 67.7 us)
Async XLA Ops:
  1.2 6.8 %collective-permute-start = (f32[16,3,1,256]{3,0,2,1:T(8,128)S(1)}, f32[16,3,1,256]{3,0,2,1:T(8,128)S(1)}, u32[]{:S(2)}, u32[]{:S(2)}) collective-permute-start(f32[16,3,1,256]{3,0,2,1:T(8,128)S(1)} %copy.193), channel_id=1, source_target_pairs={{0,2},{2,0},{1,3},{3,1},{4,6},{6,4},{5,7},{7,5},{8,10},{10,8},{9,1... | collective-permute-start | bytes 147464 | tf_op jit(solution)/shard_map/ppermute | solution.py:22
  1.3 11.4 %collective-permute-start.1 = (f32[16,3,1,256]{3,0,2,1:T(8,128)S(1)}, f32[16,3,1,256]{3,0,2,1:T(8,128)S(1)}, u32[]{:S(2)}, u32[]{:S(2)}) collective-permute-start(f32[16,3,1,256]{3,0,2,1:T(8,128)S(1)} %copy.192), channel_id=1, source_target_pairs={{2,0},{0,2},{3,1},{1,3},{6,4},{4,6},{7,5},{5,7},{10,8},{8,10},{11,... | collective-permute-start | bytes 147464 | tf_op jit(solution)/shard_map/ppermute | solution.py:23
  17.4 12.9 %copy-start.39 = (f32[32,256]{1,0:T(8,128)S(1)}, f32[32,256]{1,0:T(8,128)}, u32[]{:S(2)}) copy-start(f32[32,256]{1,0:T(8,128)} %param.7) | copy-start | bytes 98308
  25.6 2.6 copy-start.1
  28.3 7.8 %collective-permute-start.2 = (f32[16,3,34,1]{2,0,3,1:T(8,128)S(1)}, f32[16,3,34,1]{2,0,3,1:T(8,128)S(1)}, u32[]{:S(2)}, u32[]{:S(2)}) collective-permute-start(f32[16,3,34,1]{2,0,3,1:T(8,128)S(1)} %get-tuple-element.5), channel_id=1, source_target_pairs={{0,1},{1,0},{2,3},{3,2},{4,5},{5,4},{6,7},{7,6},{8,9},{9,8},{10,11... | collective-permute-start | bytes 19592 | tf_op jit(solution)/shard_map/ppermute | solution.py:22
  30.3 6.3 %collective-permute-start.3 = (f32[16,3,34,1]{2,0,3,1:T(8,128)S(1)}, f32[16,3,34,1]{2,0,3,1:T(8,128)S(1)}, u32[]{:S(2)}, u32[]{:S(2)}) collective-permute-start(f32[16,3,34,1]{2,0,3,1:T(8,128)S(1)} %get-tuple-element.6), channel_id=1, source_target_pairs={{1,0},{0,1},{3,2},{2,3},{5,4},{4,5},{7,6},{6,7},{9,8},{8,9},{11,10... | collective-permute-start | bytes 19592 | tf_op jit(solution)/shard_map/ppermute | solution.py:23
  40.7 1.3 collective-permute-start.4
  40.8 1.4 collective-permute-start.5
  45.4 4.0 collective-permute-start.6
  48.9 4.1 collective-permute-start.7
  57.5 3.4 copy-start.28
  57.5 3.4 copy-start.30
  57.5 1.8 copy-start.17
  57.5 1.9 copy-start.20
  58.0 2.9 copy-start.32
  60.9 1.3 collective-permute-start.8
  61.0 1.4 collective-permute-start.9
  65.6 3.9 collective-permute-start.10
  67.3 3.9 collective-permute-start.11
  75.6 1.5 copy-start.29
  75.6 1.7 copy-start.31
  78.7 1.3 collective-permute-start.12
  78.8 1.4 collective-permute-start.13
  81.1 16.6 %collective-permute-start.14 = (f32[16,3,34,1]{2,0,3,1:T(8,128)S(1)}, f32[16,3,34,1]{2,0,3,1:T(8,128)S(1)}, u32[]{:S(2)}, u32[]{:S(2)}) collective-permute-start(f32[16,3,34,1]{2,0,3,1:T(8,128)S(1)} %copy.180), channel_id=1, source_target_pairs={{0,1},{1,0},{2,3},{3,2},{4,5},{5,4},{6,7},{7,6},{8,9},{9,8},{10,11... | collective-permute-start | bytes 19592 | tf_op jit(solution)/shard_map/ppermute | solution.py:22
  96.2 3.9 collective-permute-start.15
  103.5 1.3 collective-permute-start.16
  103.6 1.4 collective-permute-start.17
  108.2 3.9 collective-permute-start.18
  110.0 3.9 collective-permute-start.19
  118.3 2.5 copy-start.22
  118.3 2.5 copy-start.24
  118.3 1.8 copy-start.6
  118.3 1.9 copy-start.9
  118.8 2.0 copy-start.26
  120.9 1.6 collective-permute-start.20
  120.9 1.5 collective-permute-start.21
  125.6 10.7 %collective-permute-start.22 = (f32[16,3,34,1]{2,0,3,1:T(8,128)S(1)}, f32[16,3,34,1]{2,0,3,1:T(8,128)S(1)}, u32[]{:S(2)}, u32[]{:S(2)}) collective-permute-start(f32[16,3,34,1]{2,0,3,1:T(8,128)S(1)} %copy.184), channel_id=1, source_target_pairs={{0,1},{1,0},{2,3},{3,2},{4,5},{5,4},{6,7},{7,6},{8,9},{9,8},{10,11... | collective-permute-start | bytes 19592 | tf_op jit(solution)/shard_map/ppermute | solution.py:22
  129.1 8.6 %collective-permute-start.23 = (f32[16,3,34,1]{2,0,3,1:T(8,128)S(1)}, f32[16,3,34,1]{2,0,3,1:T(8,128)S(1)}, u32[]{:S(2)}, u32[]{:S(2)}) collective-permute-start(f32[16,3,34,1]{2,0,3,1:T(8,128)S(1)} %copy.185), channel_id=1, source_target_pairs={{1,0},{0,1},{3,2},{2,3},{5,4},{4,5},{7,6},{6,7},{9,8},{8,9},{11,10... | collective-permute-start | bytes 19592 | tf_op jit(solution)/shard_map/ppermute | solution.py:23
  142.1 1.5 copy-start.23
  142.1 1.7 copy-start.25
  145.5 11.7 %copy-start.37 = (s32[32,2048]{1,0:T(8,128)S(1)}, s32[32,2048]{1,0:T(8,128)}, u32[]{:S(2)}) copy-start(s32[32,2048]{1,0:T(8,128)} %reshape.144) | copy-start | bytes 786436
  146.5 10.8 %slice-start = ((bf16[16,3,32,256]{3,0,2,1:T(8,128)(2,1)}), bf16[16,1,32,256]{3,0,2,1:T(8,128)(2,1)S(1)}, s32[]{:S(2)}) async-start(bf16[16,3,32,256]{3,0,2,1:T(8,128)(2,1)} %copy-done.34), calls=%async_computation.3 | async-start | bytes 524288 | tf_op jit(solution)/shard_map/slice | solution.py:109
  146.5 255.3 %all-to-all-start = ((bf16[16,3,32,256]{3,0,1,2:T(8,128)(2,1)}), bf16[16,3,32,256]{3,0,1,2:T(8,128)(2,1)S(1)}, u32[]{:S(2)}, u32[]{:S(2)}) async-start(bf16[16,3,32,256]{3,0,1,2:T(8,128)(2,1)} %copy.168), calls=%async_computation | async-start | bytes 1572864 | tf_op jit(solution)/shard_map/all_to_all | solution.py:121
  401.7 10.8 %copy-start.38 = (f32[1,1,2048]{2,1,0:T(1,128)S(1)}, f32[1,1,2048]{2,1,0:T(1,128)}, u32[]{:S(2)}) copy-start(f32[1,1,2048]{2,1,0:T(1,128)} %param.10) | copy-start | bytes 24580
  401.8 38.7 %all-to-all-start.1 = ((bf16[16,32,2048]{2,0,1:T(8,128)(2,1)}), bf16[16,32,2048]{2,0,1:T(8,128)(2,1)S(1)}, u32[]{:S(2)}, u32[]{:S(2)}) async-start(bf16[16,32,2048]{2,0,1:T(8,128)(2,1)} %broadcast_select_fusion), calls=%async_computation.1 | async-start | bytes 4194304 | tf_op jit(solution)/shard_map/all_to_all | solution.py:112
  441.5 2.0 copy-start.11
  459.8 2.1 copy-start.12
  459.8 2.1 copy-start.40
  (20 other events, 24.1 us)
where the time goes:
time: 501 us; the launch traced here: 491 us
  local copies, waits for them, and re-layouts  317 us (63%)
  starting transfers between devices  50.1 us (10%)
  other arithmetic  40 us (8%)
  waiting for transfers between devices  35.1 us (7%)
  matrix products  23.3 us (5%)
  blocking collectives  22.5 us (4%)
    gather x2, local copies, waits for them, and re-layouts, shards(): taken = jnp.take(height_flat, cell_index, axis=1)  242 us
    unnamed x97, local copies, waits for them, and re-layouts  31.6 us
    all_to_all x1, waiting for transfers between devices, shards(): lax.all_to_all(taken, 'mem', split_axis=1, concat_axis=0, tiled=True)  24.7 us
    all_to_all x1, blocking collectives, shards(): lax.all_to_all(updated, 'mem', split_axis=0, concat_axis=2, tiled=True)  22.5 us
    ppermute x12, starting transfers between devices, extended(): before = lax.ppermute(last, axis, up)  21.6 us
    concatenate x12, other arithmetic, extended(): array = jnp.concatenate([before, array, after], axis=dim)  20 us
    ppermute x7, local copies, waits for them, and re-layouts, extended(): after = lax.ppermute(initial, axis, down)  11.3 us
    ppermute x7, local copies, waits for them, and re-layouts, extended(): before = lax.ppermute(last, axis, up)  11.1 us
  transfers between devices with their start and end apart: 26, of which 16 were waited for; matrix products, arithmetic and copies ran while one was open for 58% of the time, Pallas kernels for 0%

commit v1 on v0

v1 whole, which is shorter than its diff:
```python
import jax
import jax.numpy as jnp
from jax import lax
from jax.experimental import pallas as pl
from jax.experimental.pallas import tpu as pltpu
from jax.sharding import PartitionSpec as P

NSI = 12
STEPS = 2
MEMBERS = 512
GROUP = 32
LOCAL = 16
CY = 32
CX = 256
SLOTS = 2048
FIELDS = 3
HALO = 6
WIDE_ROWS = CY + 2 * HALO
WIDE_COLS = CX + 128
PACK = 16
CHUNK = 512

HALF_NU = 0.35
ONE_THIRD = 1.0 / 3.0
TWO_THIRD = 2.0 / 3.0

VMEM_LIMIT = 56 << 20


def edge_lanes(block):
    lane = lax.broadcasted_iota(jnp.int32, block.shape[:-1] + (128,), block.ndim - 1)
    return jnp.where(lane < 64, block[..., :128], block[..., 128:])


def pack_edges(edges, per):
    rows = edges.shape[0]
    total = None
    for place in range(rows // per):
        part = pltpu.roll(edges[place * per : (place + 1) * per], HALO + PACK * place, 2)
        if total is None:
            total = part
        else:
            lane = lax.broadcasted_iota(jnp.int32, part.shape, 2)
            total = jnp.where(lane >= PACK * place, part, total)
    return total


def outgoing_kernel(x_ref, depth_ref, state_ref, rows_ref, cols_ref, corner_ref):
    for field in range(FIELDS):
        state_ref[field] = pltpu.einshape("mrc->rmc", x_ref[:, field])
    depth = depth_ref[...]
    outer = (slice(0, HALO), slice(CY - HALO, CY))
    for field in range(FIELDS):
        block = state_ref[field]
        edges = edge_lanes(block)
        cols_ref[4 * field : 4 * field + 4] = pack_edges(edges, 4)
        both = jnp.concatenate([edges[part] for part in outer], axis=0)
        corner_ref[2 * field : 2 * field + 2] = pack_edges(both, 2)
        rows_ref[12 * field : 12 * field + 6] = block[outer[0]]
        rows_ref[12 * field + 6 : 12 * field + 12] = block[outer[1]]
    depth_edges = edge_lanes(depth)
    cols_ref[12] = depth_edges[:16]
    cols_ref[13] = depth_edges[16:]
    rows_ref[36, 0:HALO] = depth[outer[0]]
    rows_ref[36, HALO : 2 * HALO] = depth[outer[1]]
    rows_ref[36, 2 * HALO : 16] = depth[0:4]
    corner_ref[6, 0:HALO] = depth_edges[outer[0]]
    corner_ref[6, HALO : 2 * HALO] = depth_edges[outer[1]]
    corner_ref[6, 2 * HALO : 16] = depth_edges[0:4]


def forecast_kernel(
    state_ref, depth_ref, rows_ref, cols_ref, corner_ref, cells_ref, strips_ref, base_ref, one_ref, two_ref, rate_ref
):
    upper = slice(0, HALO)
    inner = slice(HALO, HALO + CY)
    lower = slice(HALO + CY, WIDE_ROWS)
    main = slice(0, CX)
    rim = slice(CX, WIDE_COLS)

    for field in range(FIELDS):
        base_ref[field, inner, :, main] = state_ref[field]
        base_ref[field, lower, :, main] = rows_ref[12 * field : 12 * field + 6]
        base_ref[field, upper, :, main] = rows_ref[12 * field + 6 : 12 * field + 12]
        packed = cols_ref[4 * field : 4 * field + 4]
        for place in range(8):
            base_ref[field, HALO + 4 * place : HALO + 4 * place + 4, :, rim] = pltpu.roll(
                packed, 128 - HALO - PACK * place, 2
            )
        packed = corner_ref[2 * field : 2 * field + 2]
        for place in range(6):
            start = HALO + CY + 2 * place if place < 3 else 2 * place - HALO
            base_ref[field, start : start + 2, :, rim] = pltpu.roll(packed, (128 - HALO - PACK * place) % 128, 2)
    rate_ref[inner, main] = -HALF_NU * depth_ref[...]
    rate_ref[lower, main] = -HALF_NU * rows_ref[36, 0:HALO]
    rate_ref[upper, main] = -HALF_NU * rows_ref[36, HALO : 2 * HALO]
    rate_ref[HALO : HALO + 16, rim] = -HALF_NU * cols_ref[12]
    rate_ref[HALO + 16 : HALO + 32, rim] = -HALF_NU * cols_ref[13]
    rate_ref[lower, rim] = -HALF_NU * corner_ref[6, 0:HALO]
    rate_ref[upper, rim] = -HALF_NU * corner_ref[6, HALO : 2 * HALO]

    def shift_zonal(row, carry):
        base_ref[1, row] = pltpu.roll(base_ref[1, row], 1, 1)
        return carry

    lax.fori_loop(0, WIDE_ROWS, shift_zonal, 0, unroll=4)

    def advanced(source, row):
        height = source[0, row]
        zonal = source[1, row]
        divergence = (pltpu.roll(zonal, WIDE_COLS - 2, 1) - zonal) + (source[2, row + 1] - source[2, row - 1])
        height_next = height + rate_ref[pl.ds(row, 1), :] * divergence
        zonal_next = zonal + -HALF_NU * (height - pltpu.roll(height, 2, 1))
        merid_next = source[2, row] + -HALF_NU * (source[0, row + 1] - source[0, row - 1])
        return height_next, zonal_next, merid_next

    def sweep(source, target, old_part, new_part, margin):
        def step(row, carry):
            for field, value in enumerate(advanced(source, row)):
                if old_part is not None:
                    value = old_part * base_ref[field, row] + new_part * value
                target[field, row] = value
            return carry

        lax.fori_loop(margin, WIDE_ROWS - margin, step, 0, unroll=2)

    for iteration in range(STEPS):
        margin = 3 * iteration
        sweep(base_ref, one_ref, None, None, margin + 1)
        sweep(one_ref, two_ref, 0.75, 0.25, margin + 2)
        if iteration + 1 < STEPS:
            sweep(two_ref, base_ref, ONE_THIRD, TWO_THIRD, margin + 3)

    def finish(pair, carry):
        for half in range(2):
            row = 2 * pair + half
            wide = row + HALO
            height, zonal, merid = (
                ONE_THIRD * base_ref[field, wide] + TWO_THIRD * value
                for field, value in enumerate(advanced(two_ref, wide))
            )
            zonal = pltpu.roll(zonal, WIDE_COLS - 1, 1)
            height = height[:, main].astype(jnp.bfloat16)
            cells_ref[pair, :, half * CX : (half + 1) * CX] = height
            strips_ref[row, :, 0:CX] = height
            strips_ref[row, :, CX : 2 * CX] = zonal[:, main].astype(jnp.bfloat16)
            strips_ref[row, :, 2 * CX : 3 * CX] = merid[:, main].astype(jnp.bfloat16)
        return carry

    lax.fori_loop(0, CY // 2, finish, 0)


def sample_kernel(cells_ref, place_ref, out_ref):
    cells = cells_ref[...].reshape(16 * LOCAL, 2 * CX)
    for part in range(SLOTS // CHUNK):
        span = slice(part * CHUNK, (part + 1) * CHUNK)
        place = place_ref[:, span]
        within = place & (2 * CX - 1)
        pair = place >> 9
        pick = (lax.broadcasted_iota(jnp.int32, (2 * CX, CHUNK), 0) == within).astype(jnp.bfloat16)
        product = jnp.dot(cells, pick, preferred_element_type=jnp.float32)
        taken = product[:LOCAL]
        for number in range(1, 16):
            taken = jnp.where(pair == number, product[number * LOCAL : (number + 1) * LOCAL], taken)
        out_ref[0, :, span] = taken.astype(jnp.bfloat16)


def dot32(left, right, dims=((1,), (0,))):
    return lax.dot_general(left, right, (dims, ((), ())), preferred_element_type=jnp.float32)


def exact_product(matrix, column):
    high = column.astype(jnp.bfloat16)
    rest = column - high.astype(jnp.float32)
    middle = rest.astype(jnp.bfloat16)
    low = (rest - middle.astype(jnp.float32)).astype(jnp.bfloat16)
    lane = lax.broadcasted_iota(jnp.int32, (MEMBERS, 128), 1)
    wide = lambda part: jnp.broadcast_to(part.astype(jnp.float32), (MEMBERS, 128))
    parts = jnp.where(lane == 0, wide(high), jnp.where(lane == 1, wide(middle), jnp.where(lane == 2, wide(low), 0.0)))
    return jnp.sum(dot32(matrix, parts.astype(jnp.bfloat16)), axis=1, keepdims=True)


def weights_kernel(total_ref, obs_ref, values_ref, errors_ref, out_ref, dev_ref, root_ref, inverse_ref, correction_ref):
    total = total_ref[0, 0]
    projected = jnp.zeros((MEMBERS, 8), jnp.float32)
    for part in range(SLOTS // CHUNK):
        span = slice(part * CHUNK, (part + 1) * CHUNK)
        obs = obs_ref[:, span].astype(jnp.float32)
        mean = jnp.sum(obs, axis=0, keepdims=True) * (1.0 / MEMBERS)
        slot = lax.broadcasted_iota(jnp.int32, (1, CHUNK), 1) + part * CHUNK
        scale = (slot < total).astype(jnp.float32) / errors_ref[:, span]
        scaled = ((obs - mean) * scale).astype(jnp.bfloat16)
        innovation = ((values_ref[:, span] - mean) * scale).astype(jnp.bfloat16)
        dev_ref[:, span] = scaled
        rows = jnp.broadcast_to(innovation.astype(jnp.float32), (8, CHUNK)).astype(jnp.bfloat16)
        projected = projected + dot32(scaled, rows, ((1,), (1,)))
    diagonal = lax.broadcasted_iota(jnp.int32, (MEMBERS, MEMBERS), 0) == lax.broadcasted_iota(
        jnp.int32, (MEMBERS, MEMBERS), 1
    )
    system = dot32(dev_ref[...], dev_ref[...], ((1,), (1,))) + jnp.where(diagonal, MEMBERS - 1.0, 0.0)
    frob = jnp.sqrt(jnp.sum(system * system, keepdims=True))
    root = (system / frob).astype(jnp.bfloat16)
    root_ref[...] = root

    def corrected(product):
        return (jnp.where(diagonal, 1.5, 0.0) - 0.5 * product).astype(jnp.bfloat16)

    correction = corrected(root.astype(jnp.float32))
    inverse_ref[...] = correction
    root_ref[...] = dot32(root_ref[...], correction).astype(jnp.bfloat16)

    def iterate(index, carry):
        correction_ref[...] = corrected(dot32(inverse_ref[...], root_ref[...]))
        root_ref[...] = dot32(root_ref[...], correction_ref[...]).astype(jnp.bfloat16)
        inverse_ref[...] = dot32(correction_ref[...], inverse_ref[...]).astype(jnp.bfloat16)
        return carry

    lax.fori_loop(0, NSI - 2, iterate, 0)
    correction_ref[...] = corrected(dot32(inverse_ref[...], root_ref[...]))
    inverse = dot32(correction_ref[...], inverse_ref[...]).astype(jnp.bfloat16)
    inner = exact_product(inverse, projected[:, 0:1])
    mean_weights = exact_product(inverse, inner) / frob
    out_ref[...] = (jnp.sqrt((MEMBERS - 1.0) / frob) * inverse.astype(jnp.float32) + mean_weights).astype(jnp.bfloat16)


def update_kernel(weights_ref, strips_ref, out_ref):
    strips = strips_ref[...].astype(jnp.float32)
    mean = jnp.sum(strips, axis=0, keepdims=True) * (1.0 / MEMBERS)
    deviation = (strips - mean).astype(jnp.bfloat16)
    mixed = dot32(weights_ref[...], deviation, ((0,), (0,)))
    out_ref[...] = (mean + mixed).astype(jnp.bfloat16)


VMEM = pl.BlockSpec(memory_space=pltpu.VMEM)
SMEM = pl.BlockSpec(memory_space=pltpu.SMEM)


def shape(dims, kind):
    return jax.ShapeDtypeStruct(dims, kind)


def params():
    return pltpu.CompilerParams(vmem_limit_bytes=VMEM_LIMIT)


def shards(
    predicted_states,
    undisturbed_thickness_ratio,
    sampled_location,
    measured_height,
    gauge_uncertainty,
    gauge_tally,
):
    f32, bf16 = jnp.float32, jnp.bfloat16
    state, rows, cols, corner = pl.pallas_call(
        outgoing_kernel,
        out_shape=(
            shape((FIELDS, CY, LOCAL, CX), f32),
            shape((37, LOCAL, CX), f32),
            shape((14, LOCAL, 128), f32),
            shape((7, LOCAL, 128), f32),
        ),
        in_specs=[VMEM, VMEM],
        out_specs=(VMEM, VMEM, VMEM, VMEM),
        compiler_params=params(),
        name="outgoing",
    )(predicted_states, undisturbed_thickness_ratio)
    rows = lax.ppermute(rows, "ty", [(0, 1), (1, 0)])
    cols = lax.ppermute(cols, "tx", [(0, 1), (1, 0)])
    corner = lax.ppermute(corner, ("ty", "tx"), [(0, 3), (1, 2), (2, 1), (3, 0)])
    wide = (FIELDS, WIDE_ROWS, LOCAL, WIDE_COLS)
    cells, strips = pl.pallas_call(
        forecast_kernel,
        out_shape=(shape((CY // 2, LOCAL, 2 * CX), bf16), shape((CY, LOCAL, FIELDS * CX), bf16)),
        in_specs=[VMEM] * 5,
        out_specs=(VMEM, VMEM),
        scratch_shapes=[pltpu.VMEM(wide, f32)] * 3 + [pltpu.VMEM((WIDE_ROWS + 4, WIDE_COLS), f32)],
        compiler_params=params(),
        name="forecast",
    )(state, undisturbed_thickness_ratio, rows, cols, corner)
    taken = pl.pallas_call(
        sample_kernel,
        grid=(GROUP,),
        out_shape=shape((GROUP, LOCAL, SLOTS), bf16),
        in_specs=[
            pl.BlockSpec((CY // 2, LOCAL, 2 * CX), lambda region: (0, 0, 0)),
            pl.BlockSpec((1, SLOTS), lambda region: (0, region)),
        ],
        out_specs=pl.BlockSpec((1, LOCAL, SLOTS), lambda region: (region, 0, 0)),
        compiler_params=params(),
        name="sample",
    )(cells, sampled_location.reshape(1, GROUP * SLOTS))
    gathered = lax.all_to_all(taken, "mem", 0, 0, tiled=True).reshape(MEMBERS, SLOTS)
    weights = pl.pallas_call(
        weights_kernel,
        out_shape=shape((MEMBERS, MEMBERS), bf16),
        in_specs=[SMEM, VMEM, VMEM, VMEM],
        out_specs=VMEM,
        scratch_shapes=[pltpu.VMEM((MEMBERS, SLOTS), bf16)] + [pltpu.VMEM((MEMBERS, MEMBERS), bf16)] * 3,
        compiler_params=params(),
        name="weights",
    )(
        gauge_tally.reshape(1, 1),
        gathered,
        measured_height.reshape(1, SLOTS),
        gauge_uncertainty.reshape(1, SLOTS),
    )
    regrouped = lax.all_to_all(strips, "mem", 0, 0, tiled=True).reshape(MEMBERS, FIELDS * CX)
    updated = pl.pallas_call(
        update_kernel,
        out_shape=shape((MEMBERS, FIELDS * CX), bf16),
        in_specs=[VMEM, VMEM],
        out_specs=VMEM,
        compiler_params=params(),
        name="update",
    )(weights, regrouped)
    back = lax.all_to_all(updated.reshape(GROUP, LOCAL, FIELDS * CX), "mem", 0, 0, tiled=True)
    return back.reshape(CY, LOCAL, FIELDS, CX).transpose(1, 2, 0, 3)


def solution(mesh):
    in_specs = (
        P("mem", None, "ty", "tx"),
        P("ty", "tx"),
        P("ty", "tx", None),
        P("ty", "tx", "mem"),
        P("ty", "tx", "mem"),
        P("ty", "tx", "mem"),
    )
    out_specs = P("mem", None, "ty", "tx")
    return jax.shard_map(shards, mesh=mesh, in_specs=in_specs, out_specs=out_specs, check_vma=False)
```

time: 501 us -> 150 us (0.30); the launches traced: 491 us -> 150 us
  local copies, waits for them, and re-layouts: 317 us -> 3.54 us
  Pallas kernels: 0 us -> 69.3 us
  starting transfers between devices: 50.1 us -> 7.07 us
  blocking collectives: 22.5 us -> 64.1 us
  other arithmetic: 40 us -> 0 us
  waiting for transfers between devices: 35.1 us -> 4.96 us
  matrix products: 23.3 us -> 0 us
    gather x2 -> x0, local copies, waits for them, and re-layouts: 242 us -> none  [shards(): taken = jnp.take(height_flat, cell_index, axis=1)]
    pallas_call x0 -> x5, Pallas kernels: none -> 69.3 us  [the longest x1 29.1 us: shards(): pl.pallas_call(sample_kernel, grid=(GROUP,), out_shape=shape((GROUP, LOCA...]
    all_to_all x1 -> x2, blocking collectives: 22.5 us -> 64.1 us  [the longest x1 39.9 us: shards(): lax.all_to_all(taken, 'mem', 0, 0, tiled=True).reshape(MEMBERS, SLOTS)]
    unnamed x97 -> x8, local copies, waits for them, and re-layouts: 31.6 us -> 1.74 us
    ppermute x24 -> x3, starting transfers between devices: 29.3 us -> 2.15 us  [the longest x1 2.03 us: shards(): cols = lax.ppermute(cols, 'tx', [(0, 1), (1, 0)])]
    all_to_all x2 -> x1, waiting for transfers between devices: 24.7 us -> 0.01 us  [shards(): lax.all_to_all(strips, 'mem', 0, 0, tiled=True)]
    dot_general x39 -> x0, matrix products: 23.3 us -> none  [the longest x12 7.86 us: transform_weights(): jnp.dot(correction, inverse_root, preferred_element_type=jnp.float32)]
    ppermute x14 -> x0, local copies, waits for them, and re-layouts: 22.4 us -> none  [the longest x7 11.3 us: extended(): after = lax.ppermute(initial, axis, down)]
  transfers between devices with their start and end apart: 26 -> 4, of which waited for: 16 -> 1; matrix products, arithmetic and copies ran while one was open for 58% -> 0% of each run, Pallas kernels for 0% -> 12%
where the time goes in v1:
time: 150 us
  Pallas kernels  69.3 us (46%)
  blocking collectives  64.1 us (43%)
  starting transfers between devices  7.07 us (5%)
  waiting for transfers between devices  4.96 us (3%)
  local copies, waits for them, and re-layouts  3.54 us (2%)
    all_to_all x1, blocking collectives, shards(): lax.all_to_all(taken, 'mem', 0, 0, tiled=True).reshape(MEMBERS, SLOTS)  39.9 us
    pallas_call x1, Pallas kernels, shards(): pl.pallas_call(sample_kernel, grid=(GROUP,), out_shape=shape((GROUP, LOCA...  29.1 us
    all_to_all x1, blocking collectives, shards(): lax.all_to_all(updated.reshape(GROUP, LOCAL, FIELDS * CX), 'mem', 0, 0, t...  24.2 us
    pallas_call x1, Pallas kernels, shards(): pl.pallas_call(weights_kernel, out_shape=shape((MEMBERS, MEMBERS), bf16),...  18 us
    pallas_call x1, Pallas kernels, shards(): pl.pallas_call(forecast_kernel, out_shape=(shape((CY // 2, LOCAL, 2 * CX)...  16.1 us
    ppermute x1, waiting for transfers between devices, shards(): lax.ppermute(corner, ('ty', 'tx'), [(0, 3), (1, 2), (2, 1), (3, 0)])  4.95 us
    all_to_all x1, starting transfers between devices, shards(): lax.all_to_all(strips, 'mem', 0, 0, tiled=True)  4.93 us
    pallas_call x1, Pallas kernels, shards(): pl.pallas_call(outgoing_kernel, out_shape=(shape((FIELDS, CY, LOCAL, CX),...  3.13 us
  transfers between devices with their start and end apart: 4, of which 1 were waited for; matrix products, arithmetic and copies ran while one was open for 0% of the time, Pallas kernels for 12%

profile of v1, /device:TPU:0, one launch (start us, length us, event | category | flops | bytes accessed | tf_op | source)
XLA Modules:
  0.0 149.6 jit_solution(8630656821040339459)
XLA Ops:
  0.0 3.1 %outgoing.1 = (f32[3,32,16,256]{3,2,1,0:T(8,128)}, f32[37,16,256]{2,1,0:T(8,128)}, f32[14,16,128]{2,1,0:T(8,128)}, f32[7,16,128]{2,1,0:T(8,128)}) custom-call(f32[16,3,32,256]{3,2,1,0:T(8,128)} %x_ref.1, f32[32,256]{1,0:T(8,128)} %depth_ref.3), custom_call_target="tpu_custom_call" | custom-call | tf_op jit(solution)/shard_map/outgoing/pallas_call | solution.py:255
  3.1 0.0 collective-permute-start
  3.1 2.0 %collective-permute-start.1 = (f32[14,16,128]{2,1,0:T(8,128)}, f32[14,16,128]{2,1,0:T(8,128)S(1)}, u32[]{:S(2)}, u32[]{:S(2)}) collective-permute-start(f32[14,16,128]{2,1,0:T(8,128)} %get-tuple-element.13), channel_id=1, source_target_pairs={{0,1},{1,0},{2,3},{3,2},{4,5},{5,4},{6,7},{7,6},{8,9},{9,8},{10,11... | collective-permute-start | bytes 344072 | tf_op jit(solution)/shard_map/ppermute | solution.py:269
  5.2 0.1 collective-permute-start.2
  5.3 5.0 %collective-permute-done.2.corner_ref = f32[7,16,128]{2,1,0:T(8,128)S(1)} collective-permute-done((f32[7,16,128]{2,1,0:T(8,128)}, f32[7,16,128]{2,1,0:T(8,128)S(1)}, u32[]{:S(2)}, u32[]{:S(2)}) %collective-permute-start.2) | collective-permute-done | bytes 57376 | tf_op jit(solution)/shard_map/ppermute | solution.py:270
  10.2 0.0 copy-start.3
  10.2 0.0 collective-permute-done.1.cols_ref
  10.2 0.0 copy-start.2
  10.2 0.0 collective-permute-done.rows_ref
  10.2 0.0 copy-start.1
  10.3 0.6 copy-done.3
  10.9 0.0 copy-done.2
  10.9 0.2 copy-done.1
  11.1 16.1 %forecast.1 = (bf16[16,16,512]{2,1,0:T(8,128)(2,1)}, bf16[32,16,768]{2,1,0:T(8,128)(2,1)}) custom-call(f32[3,32,16,256]{3,2,1,0:T(8,128)} %get-tuple-element.11.state_ref, f32[32,256]{1,0:T(8,128)} %depth_ref.3, f32[37,16,256]{2,1,0:T(8,128)} %copy-done.1, f32[14,16,128]{2,1,0:T(8,128)} %copy-done.2, f32[7,16,128]{2,1,0:T(8,128)} %copy-done.3), custom_call_target="tpu_custom_call" | custom-call | tf_op jit(solution)/shard_map/forecast/pallas_call | solution.py:272
  27.2 29.1 %sample.1 = bf16[32,16,2048]{2,1,0:T(8,128)(2,1)} custom-call(bf16[16,16,512]{2,1,0:T(8,128)(2,1)} %get-tuple-element.15.cells_ref, s32[1,65536]{1,0:T(1,128)} %bitcast.13), custom_call_target="tpu_custom_call" | custom-call | tf_op jit(solution)/shard_map/sample/pallas_call | solution.py:281
  56.3 39.9 %all_to_all.15 = bf16[32,16,2048]{2,1,0:T(8,128)(2,1)} all-to-all(bf16[32,16,2048]{2,1,0:T(8,128)(2,1)} %sample.1), channel_id=1, replica_groups=mesh['mem'=32,'ty'=2,'tx'=2] {'mem'}, dimensions={0} | all-to-all | bytes 4194304 | tf_op jit(solution)/shard_map/all_to_all | solution.py:293
  96.2 4.9 %all-to-all-start.1 = ((bf16[32,16,768]{2,1,0:T(8,128)(2,1)}), bf16[32,16,768]{2,1,0:T(8,128)(2,1)S(1)}, u32[]{:S(2)}, u32[]{:S(2)}) async-start(bf16[32,16,768]{2,1,0:T(8,128)(2,1)} %get-tuple-element.16), calls=%async_computation.1 | async-start | bytes 1572864 | tf_op jit(solution)/shard_map/all_to_all | solution.py:308
  101.8 18.0 %weights.1.weights_ref = bf16[512,512]{1,0:T(8,128)(2,1)} custom-call(s32[1,1]{1,0:T(1,128)} %bitcast.8.total_ref, bf16[512,2048]{1,0:T(8,128)(2,1)} %bitcast.9, f32[1,2048]{1,0:T(1,128)} %bitcast.14, f32[1,2048]{1,0:T(1,128)} %bitcast.15), custom_call_target="tpu_custom_call" | custom-call | tf_op jit(solution)/shard_map/weights/pallas_call | solution.py:294
  119.8 0.0 all-to-all-done.1
  119.8 0.0 copy-start
  119.8 0.9 copy-done
  120.7 2.9 %update.1 = bf16[512,768]{1,0:T(8,128)(2,1)} custom-call(bf16[512,512]{1,0:T(8,128)(2,1)} %weights.1.weights_ref, bf16[512,768]{1,0:T(8,128)(2,1)} %bitcast.11), custom_call_target="tpu_custom_call" | custom-call | tf_op jit(solution)/shard_map/update/pallas_call | solution.py:309
  123.6 24.2 %all_to_all.16 = bf16[32,16,768]{2,1,0:T(8,128)(2,1)S(1)} all-to-all(bf16[32,16,768]{2,1,0:T(8,128)(2,1)} %bitcast.12), channel_id=1, replica_groups=mesh['mem'=32,'ty'=2,'tx'=2] {'mem'}, dimensions={0} | all-to-all | bytes 1572864 | tf_op jit(solution)/shard_map/all_to_all | solution.py:317
  147.8 0.3 reshape.31
  148.2 1.5 copy.7
Async XLA Ops:
  3.1 7.1 %collective-permute-start = (f32[37,16,256]{2,1,0:T(8,128)}, f32[37,16,256]{2,1,0:T(8,128)S(1)}, u32[]{:S(2)}, u32[]{:S(2)}) collective-permute-start(f32[37,16,256]{2,1,0:T(8,128)} %get-tuple-element.12), channel_id=1, source_target_pairs={{0,2},{2,0},{1,3},{3,1},{4,6},{6,4},{5,7},{7,5},{8,10},{10,8},{9,1... | collective-permute-start | bytes 1818632 | tf_op jit(solution)/shard_map/ppermute | solution.py:268
  3.1 7.1 %collective-permute-start.1 = (f32[14,16,128]{2,1,0:T(8,128)}, f32[14,16,128]{2,1,0:T(8,128)S(1)}, u32[]{:S(2)}, u32[]{:S(2)}) collective-permute-start(f32[14,16,128]{2,1,0:T(8,128)} %get-tuple-element.13), channel_id=1, source_target_pairs={{0,1},{1,0},{2,3},{3,2},{4,5},{5,4},{6,7},{7,6},{8,9},{9,8},{10,11... | collective-permute-start | bytes 344072 | tf_op jit(solution)/shard_map/ppermute | solution.py:269
  5.2 5.1 %collective-permute-start.2 = (f32[7,16,128]{2,1,0:T(8,128)}, f32[7,16,128]{2,1,0:T(8,128)S(1)}, u32[]{:S(2)}, u32[]{:S(2)}) collective-permute-start(f32[7,16,128]{2,1,0:T(8,128)} %get-tuple-element.14), channel_id=1, source_target_pairs={{0,3},{1,2},{2,1},{3,0},{4,7},{5,6},{6,5},{7,4},{8,11},{9,10},{10,... | collective-permute-start | bytes 172040 | tf_op jit(solution)/shard_map/ppermute | solution.py:270
  10.2 0.6 copy-start.3
  10.2 0.7 copy-start.2
  10.2 0.9 copy-start.1
  96.2 23.6 %all-to-all-start.1 = ((bf16[32,16,768]{2,1,0:T(8,128)(2,1)}), bf16[32,16,768]{2,1,0:T(8,128)(2,1)S(1)}, u32[]{:S(2)}, u32[]{:S(2)}) async-start(bf16[32,16,768]{2,1,0:T(8,128)(2,1)} %get-tuple-element.16), calls=%async_computation.1 | async-start | bytes 1572864 | tf_op jit(solution)/shard_map/all_to_all | solution.py:308
  119.8 0.9 copy-start

commit v2 on v1

--- a/solution.py
+++ b/solution.py
@@ -14,17 +14,18 @@
 CX = 256
 SLOTS = 2048
 FIELDS = 3
+BUNDLE = SLOTS + FIELDS * CX
 HALO = 6
 WIDE_ROWS = CY + 2 * HALO
 WIDE_COLS = CX + 128
 PACK = 16
 CHUNK = 512
+PRODUCT = 1536
+BY_LANES = (2, 1, 1)
 
 HALF_NU = 0.35
 ONE_THIRD = 1.0 / 3.0
 TWO_THIRD = 2.0 / 3.0
-
-VMEM_LIMIT = 56 << 20
 
 
 def edge_lanes(block):
@@ -45,12 +46,12 @@
     return total
 
 
-def outgoing_kernel(x_ref, depth_ref, state_ref, rows_ref, cols_ref, corner_ref):
+def outgoing_kernel(x_ref, depth_in_ref, state_ref, depth_ref, rows_ref, cols_ref, corner_ref):
+    depth = depth_in_ref[...]
+    depth_ref[...] = depth
+    outer = (slice(0, HALO), slice(CY - HALO, CY))
     for field in range(FIELDS):
         state_ref[field] = pltpu.einshape("mrc->rmc", x_ref[:, field])
-    depth = depth_ref[...]
-    outer = (slice(0, HALO), slice(CY - HALO, CY))
-    for field in range(FIELDS):
         block = state_ref[field]
         edges = edge_lanes(block)
         cols_ref[4 * field : 4 * field + 4] = pack_edges(edges, 4)
@@ -103,7 +104,7 @@
         base_ref[1, row] = pltpu.roll(base_ref[1, row], 1, 1)
         return carry
 
-    lax.fori_loop(0, WIDE_ROWS, shift_zonal, 0, unroll=4)
+    lax.fori_loop(0, WIDE_ROWS, shift_zonal, 0, unroll=11)
 
     def advanced(source, row):
         height = source[0, row]
@@ -122,7 +123,7 @@
                 target[field, row] = value
             return carry
 
-        lax.fori_loop(margin, WIDE_ROWS - margin, step, 0, unroll=2)
+        lax.fori_loop(margin, WIDE_ROWS - margin, step, 0, unroll=8)
 
     for iteration in range(STEPS):
         margin = 3 * iteration
@@ -147,22 +148,54 @@
             strips_ref[row, :, 2 * CX : 3 * CX] = merid[:, main].astype(jnp.bfloat16)
         return carry
 
-    lax.fori_loop(0, CY // 2, finish, 0)
-
-
-def sample_kernel(cells_ref, place_ref, out_ref):
+    lax.fori_loop(0, CY // 2, finish, 0, unroll=4)
+
+
+def sample_kernel(cells_ref, strips_ref, place_ref, out_ref, halves_ref):
+    out_ref[0, :, SLOTS:] = strips_ref[0]
+
+    @pl.when(pl.program_id(0) == 0)
+    def _():
+        def widen(pair, carry):
+            for quarter in range(4):
+                halves_ref[4 * pair + quarter] = cells_ref[pair, :, quarter * 128 : (quarter + 1) * 128].astype(jnp.float32)
+            return carry
+
+        lax.fori_loop(0, 16, widen, 0)
+
     cells = cells_ref[...].reshape(16 * LOCAL, 2 * CX)
-    for part in range(SLOTS // CHUNK):
-        span = slice(part * CHUNK, (part + 1) * CHUNK)
+
+    def by_product(start, width):
+        span = slice(start, start + width)
         place = place_ref[:, span]
         within = place & (2 * CX - 1)
         pair = place >> 9
-        pick = (lax.broadcasted_iota(jnp.int32, (2 * CX, CHUNK), 0) == within).astype(jnp.bfloat16)
+        hit = lax.broadcasted_iota(jnp.int16, (2 * CX, width), 0) == within.astype(jnp.int16)
+        pick = jnp.where(hit, jnp.ones(hit.shape, jnp.bfloat16), jnp.zeros(hit.shape, jnp.bfloat16))
         product = jnp.dot(cells, pick, preferred_element_type=jnp.float32)
         taken = product[:LOCAL]
         for number in range(1, 16):
             taken = jnp.where(pair == number, product[number * LOCAL : (number + 1) * LOCAL], taken)
         out_ref[0, :, span] = taken.astype(jnp.bfloat16)
+
+    def by_lanes(start):
+        span = slice(start, start + 128)
+        place = place_ref[:, span]
+        lane = jnp.broadcast_to(place & 127, (8, 128))
+        block = jnp.broadcast_to(place >> 7, (8, 128))
+        taken = [jnp.zeros((8, 128), jnp.float32)] * 2
+        for number in range(64):
+            match = block == number
+            for half in range(2):
+                source = halves_ref[number, 8 * half : 8 * half + 8, :]
+                moved = jnp.take_along_axis(source, lane, axis=1, mode="promise_in_bounds")
+                taken[half] = jnp.where(match, moved, taken[half])
+        out_ref[0, :, span] = jnp.concatenate(taken, axis=0).astype(jnp.bfloat16)
+
+    for part in range(PRODUCT // CHUNK):
+        by_product(part * CHUNK, CHUNK)
+        for piece in range(BY_LANES[part]):
+            by_lanes(PRODUCT + 128 * (sum(BY_LANES[:part]) + piece))
 
 
 def dot32(left, right, dims=((1,), (0,))):
@@ -180,12 +213,14 @@
     return jnp.sum(dot32(matrix, parts.astype(jnp.bfloat16)), axis=1, keepdims=True)
 
 
-def weights_kernel(total_ref, obs_ref, values_ref, errors_ref, out_ref, dev_ref, root_ref, inverse_ref, correction_ref):
+def analysis_kernel(
+    total_ref, gathered_ref, values_ref, errors_ref, out_ref, dev_ref, root_ref, inverse_ref, correction_ref
+):
     total = total_ref[0, 0]
     projected = jnp.zeros((MEMBERS, 8), jnp.float32)
     for part in range(SLOTS // CHUNK):
         span = slice(part * CHUNK, (part + 1) * CHUNK)
-        obs = obs_ref[:, span].astype(jnp.float32)
+        obs = gathered_ref[:, span].astype(jnp.float32)
         mean = jnp.sum(obs, axis=0, keepdims=True) * (1.0 / MEMBERS)
         slot = lax.broadcasted_iota(jnp.int32, (1, CHUNK), 1) + part * CHUNK
         scale = (slot < total).astype(jnp.float32) / errors_ref[:, span]
@@ -220,15 +255,19 @@
     inverse = dot32(correction_ref[...], inverse_ref[...]).astype(jnp.bfloat16)
     inner = exact_product(inverse, projected[:, 0:1])
     mean_weights = exact_product(inverse, inner) / frob
-    out_ref[...] = (jnp.sqrt((MEMBERS - 1.0) / frob) * inverse.astype(jnp.float32) + mean_weights).astype(jnp.bfloat16)
-
-
-def update_kernel(weights_ref, strips_ref, out_ref):
-    strips = strips_ref[...].astype(jnp.float32)
-    mean = jnp.sum(strips, axis=0, keepdims=True) * (1.0 / MEMBERS)
-    deviation = (strips - mean).astype(jnp.bfloat16)
-    mixed = dot32(weights_ref[...], deviation, ((0,), (0,)))
-    out_ref[...] = (mean + mixed).astype(jnp.bfloat16)
+    root_ref[...] = (jnp.sqrt((MEMBERS - 1.0) / frob) * inverse.astype(jnp.float32) + mean_weights).astype(jnp.bfloat16)
+    for part in range(FIELDS):
+        span = slice(part * CX, (part + 1) * CX)
+        strips = gathered_ref[:, SLOTS + part * CX : SLOTS + (part + 1) * CX].astype(jnp.float32)
+        field_mean = jnp.sum(strips, axis=0, keepdims=True) * (1.0 / MEMBERS)
+        deviation = (strips - field_mean).astype(jnp.bfloat16)
+        mixed = dot32(root_ref[...], deviation, ((0,), (0,)))
+        out_ref[:, span] = (field_mean + mixed).astype(jnp.bfloat16)
+
+
+def deliver_kernel(back_ref, out_ref):
+    for field in range(FIELDS):
+        out_ref[:, field] = pltpu.einshape("rmc->mrc", back_ref[:, :, field * CX : (field + 1) * CX])
 
 
 VMEM = pl.BlockSpec(memory_space=pltpu.VMEM)
@@ -239,8 +278,8 @@
     return jax.ShapeDtypeStruct(dims, kind)
 
 
-def params():
-    return pltpu.CompilerParams(vmem_limit_bytes=VMEM_LIMIT)
+def params(mebibytes):
+    return pltpu.CompilerParams(vmem_limit_bytes=mebibytes << 20)
 
 
 def shards(
@@ -252,17 +291,18 @@
     gauge_tally,
 ):
     f32, bf16 = jnp.float32, jnp.bfloat16
-    state, rows, cols, corner = pl.pallas_call(
+    state, depth, rows, cols, corner = pl.pallas_call(
         outgoing_kernel,
         out_shape=(
             shape((FIELDS, CY, LOCAL, CX), f32),
+            shape((CY, CX), f32),
             shape((37, LOCAL, CX), f32),
             shape((14, LOCAL, 128), f32),
             shape((7, LOCAL, 128), f32),
         ),
         in_specs=[VMEM, VMEM],
-        out_specs=(VMEM, VMEM, VMEM, VMEM),
-        compiler_params=params(),
+        out_specs=(VMEM,) * 5,
+        compiler_params=params(12),
         name="outgoing",
     )(predicted_states, undisturbed_thickness_ratio)
     rows = lax.ppermute(rows, "ty", [(0, 1), (1, 0)])
@@ -275,47 +315,47 @@
         in_specs=[VMEM] * 5,
         out_specs=(VMEM, VMEM),
         scratch_shapes=[pltpu.VMEM(wide, f32)] * 3 + [pltpu.VMEM((WIDE_ROWS + 4, WIDE_COLS), f32)],
-        compiler_params=params(),
+        compiler_params=params(20),
         name="forecast",
-    )(state, undisturbed_thickness_ratio, rows, cols, corner)
+    )(state, depth, rows, cols, corner)
     taken = pl.pallas_call(
         sample_kernel,
         grid=(GROUP,),
-        out_shape=shape((GROUP, LOCAL, SLOTS), bf16),
+        out_shape=shape((GROUP, LOCAL, BUNDLE), bf16),
         in_specs=[
             pl.BlockSpec((CY // 2, LOCAL, 2 * CX), lambda region: (0, 0, 0)),
+            pl.BlockSpec((1, LOCAL, FIELDS * CX), lambda region: (region, 0, 0)),
             pl.BlockSpec((1, SLOTS), lambda region: (0, region)),
         ],
-        out_specs=pl.BlockSpec((1, LOCAL, SLOTS), lambda region: (region, 0, 0)),
-        compiler_params=params(),
+        out_specs=pl.BlockSpec((1, LOCAL, BUNDLE), lambda region: (region, 0, 0)),
+        scratch_shapes=[pltpu.VMEM((64, LOCAL, 128), jnp.float32)],
+        compiler_params=params(52),
         name="sample",
-    )(cells, sampled_location.reshape(1, GROUP * SLOTS))
-    gathered = lax.all_to_all(taken, "mem", 0, 0, tiled=True).reshape(MEMBERS, SLOTS)
-    weights = pl.pallas_call(
-        weights_kernel,
-        out_shape=shape((MEMBERS, MEMBERS), bf16),
+    )(cells, strips, sampled_location.reshape(1, GROUP * SLOTS))
+    gathered = lax.all_to_all(taken, "mem", 0, 0, tiled=True).reshape(MEMBERS, BUNDLE)
+    updated = pl.pallas_call(
+        analysis_kernel,
+        out_shape=shape((MEMBERS, FIELDS * CX), bf16),
         in_specs=[SMEM, VMEM, VMEM, VMEM],
         out_specs=VMEM,
         scratch_shapes=[pltpu.VMEM((MEMBERS, SLOTS), bf16)] + [pltpu.VMEM((MEMBERS, MEMBERS), bf16)] * 3,
-        compiler_params=params(),
-        name="weights",
+        compiler_params=params(24),
+        name="analysis",
     )(
         gauge_tally.reshape(1, 1),
         gathered,
         measured_height.reshape(1, SLOTS),
         gauge_uncertainty.reshape(1, SLOTS),
     )
-    regrouped = lax.all_to_all(strips, "mem", 0, 0, tiled=True).reshape(MEMBERS, FIELDS * CX)
-    updated = pl.pallas_call(
-        update_kernel,
-        out_shape=shape((MEMBERS, FIELDS * CX), bf16),
-        in_specs=[VMEM, VMEM],
+    back = lax.all_to_all(updated.reshape(GROUP, LOCAL, FIELDS * CX), "mem", 0, 0, tiled=True)
+    return pl.pallas_call(
+        deliver_kernel,
+        out_shape=shape((LOCAL, FIELDS, CY, CX), bf16),
+        in_specs=[VMEM],
         out_specs=VMEM,
-        compiler_params=params(),
-        name="update",
-    )(weights, regrouped)
-    back = lax.all_to_all(updated.reshape(GROUP, LOCAL, FIELDS * CX), "mem", 0, 0, tiled=True)
-    return back.reshape(CY, LOCAL, FIELDS, CX).transpose(1, 2, 0, 3)
+        compiler_params=params(8),
+        name="deliver",
+    )(back)
 
 
 def solution(mesh):

time: 150 us -> 128 us (0.85)
  blocking collectives: 64.1 us -> 22.7 us
  waiting for transfers between devices: 4.96 us -> 43.1 us
  Pallas kernels: 69.3 us -> 45.9 us
  starting transfers between devices: 7.07 us -> 12.5 us
    all_to_all x1 -> x0, blocking collectives: 39.9 us -> none  [shards(): lax.all_to_all(taken, 'mem', 0, 0, tiled=True).reshape(MEMBERS, SLOTS)]
    all_to_all x1, waiting for transfers between devices: 0.01 us -> 38.5 us  [shards(): lax.all_to_all(taken, 'mem', 0, 0, tiled=True).reshape(MEMBERS, BUNDLE)]
    pallas_call x1, Pallas kernels: 16.1 us -> 7.6 us  [shards(): pl.pallas_call(forecast_kernel, out_shape=(shape((CY // 2, LOCAL, 2 * CX)...]
    pallas_call x1, Pallas kernels: 29.1 us -> 20.5 us  [shards(): pl.pallas_call(sample_kernel, grid=(GROUP,), out_shape=shape((GROUP, LOCA...]
    all_to_all x1, starting transfers between devices: 4.93 us -> 10.3 us  [shards(): lax.all_to_all(taken, 'mem', 0, 0, tiled=True).reshape(MEMBERS, BUNDLE)]
    pallas_call x2, Pallas kernels: 20.9 us -> 17.3 us  [the longest x1 16.3 us: shards(): pl.pallas_call(analysis_kernel, out_shape=shape((MEMBERS, FIELDS * CX), b...]
    pallas_call x1, Pallas kernels: 3.13 us -> 0.43 us  [shards(): pl.pallas_call(outgoing_kernel, out_shape=(shape((FIELDS, CY, LOCAL, CX),...]
  transfers between devices with their start and end apart: 4 -> 4, of which waited for: 1 -> 2; matrix products, arithmetic and copies ran while one was open for 0% -> 0% of each run, Pallas kernels for 12% -> 0%
where the time goes in v2:
time: 128 us; the launch traced here: 127 us
  Pallas kernels  45.9 us (36%)
  waiting for transfers between devices  43.1 us (34%)
  blocking collectives  22.7 us (18%)
  starting transfers between devices  12.5 us (10%)
  local copies, waits for them, and re-layouts  2.18 us (2%)
    all_to_all x1, waiting for transfers between devices, shards(): lax.all_to_all(taken, 'mem', 0, 0, tiled=True).reshape(MEMBERS, BUNDLE)  38.5 us
    all_to_all x1, blocking collectives, shards(): lax.all_to_all(updated.reshape(GROUP, LOCAL, FIELDS * CX), 'mem', 0, 0, t...  22.7 us
    pallas_call x1, Pallas kernels, shards(): pl.pallas_call(sample_kernel, grid=(GROUP,), out_shape=shape((GROUP, LOCA...  20.5 us
    pallas_call x1, Pallas kernels, shards(): pl.pallas_call(analysis_kernel, out_shape=shape((MEMBERS, FIELDS * CX), b...  16.3 us
    all_to_all x1, starting transfers between devices, shards(): lax.all_to_all(taken, 'mem', 0, 0, tiled=True).reshape(MEMBERS, BUNDLE)  10.3 us
    pallas_call x1, Pallas kernels, shards(): pl.pallas_call(forecast_kernel, out_shape=(shape((CY // 2, LOCAL, 2 * CX)...  7.6 us
    ppermute x1, waiting for transfers between devices, shards(): lax.ppermute(corner, ('ty', 'tx'), [(0, 3), (1, 2), (2, 1), (3, 0)])  4.65 us
  transfers between devices with their start and end apart: 4, of which 2 were waited for; matrix products, arithmetic and copies ran while one was open for 0% of the time, Pallas kernels for 0%

profile of v2, /device:TPU:0, one launch (start us, length us, event | category | flops | bytes accessed | tf_op | source)
XLA Modules:
  0.0 127.2 jit_solution(17477126009992295295)
XLA Ops:
  0.0 0.0 copy-start
  0.0 1.4 %copy-done = f32[16,3,32,256]{3,2,1,0:T(8,128)S(1)} copy-done((f32[16,3,32,256]{3,2,1,0:T(8,128)S(1)}, f32[16,3,32,256]{3,2,1,0:T(8,128)}, u32[]{:S(2)}) %copy-start) | copy-done | bytes 1572888
  1.4 0.0 copy-start.2
  1.4 0.8 copy-done.2
  2.2 0.0 copy-start.1
  2.2 0.4 outgoing.1
  2.6 0.1 collective-permute-start
  2.7 2.1 %collective-permute-start.1 = (f32[14,16,128]{2,1,0:T(8,128)S(1)}, f32[14,16,128]{2,1,0:T(8,128)S(1)}, u32[]{:S(2)}, u32[]{:S(2)}) collective-permute-start(f32[14,16,128]{2,1,0:T(8,128)S(1)} %get-tuple-element.15), channel_id=1, source_target_pairs={{0,1},{1,0},{2,3},{3,2},{4,5},{5,4},{6,7},{7,6},{8,9},{9,8},{10,11... | collective-permute-start | bytes 344072 | tf_op jit(solution)/shard_map/ppermute | solution.py:309
  4.8 0.0 collective-permute-start.2
  4.8 4.6 %collective-permute-done.2.corner_ref = f32[7,16,128]{2,1,0:T(8,128)S(1)} collective-permute-done((f32[7,16,128]{2,1,0:T(8,128)S(1)}, f32[7,16,128]{2,1,0:T(8,128)S(1)}, u32[]{:S(2)}, u32[]{:S(2)}) %collective-permute-start.2) | collective-permute-done | bytes 57376 | tf_op jit(solution)/shard_map/ppermute | solution.py:310
  9.5 0.0 collective-permute-done.1.cols_ref
  9.5 0.0 collective-permute-done.rows_ref
  9.5 7.6 %forecast.1 = (bf16[16,16,512]{2,1,0:T(8,128)(2,1)S(1)}, bf16[32,16,768]{2,1,0:T(8,128)(2,1)S(1)}) custom-call(f32[3,32,16,256]{3,2,1,0:T(8,128)S(1)} %get-tuple-element.12.state_ref, f32[32,256]{1,0:T(8,128)S(1)} %get-tuple-element.13.depth_ref, f32[37,16,256]{2,1,0:T(8,128)S(1)} %collective-permute-done.rows_ref, ...), custom_call_target="tpu_custom_call" | custom-call | tf_op jit(solution)/shard_map/forecast/pallas_call | solution.py:312
  17.1 0.0 copy-done.1
  17.1 20.5 %sample.1 = bf16[32,16,2816]{2,1,0:T(8,128)(2,1)} custom-call(bf16[16,16,512]{2,1,0:T(8,128)(2,1)S(1)} %get-tuple-element.17.cells_ref, bf16[32,16,768]{2,1,0:T(8,128)(2,1)S(1)} %get-tuple-element.18.strips_ref, s32[1,65536]{1,0:T(1,128)S(1)} %bitcast.9), custom_call_target="tpu_custom_call" | custom-call | tf_op jit(solution)/shard_map/sample/pallas_call | solution.py:321
  37.6 0.0 copy-start.3
  37.6 0.0 copy-start.4
  37.7 10.3 %all-to-all-start = ((bf16[32,16,2816]{2,1,0:T(8,128)(2,1)}), bf16[32,16,2816]{2,1,0:T(8,128)(2,1)S(1)}, u32[]{:S(2)}, u32[]{:S(2)}) async-start(bf16[32,16,2816]{2,1,0:T(8,128)(2,1)} %sample.1), calls=%async_computation | async-start | bytes 5767168 | tf_op jit(solution)/shard_map/all_to_all | solution.py:335
  48.6 38.5 %all-to-all-done = bf16[32,16,2816]{2,1,0:T(8,128)(2,1)S(1)} async-done(((bf16[32,16,2816]{2,1,0:T(8,128)(2,1)}), bf16[32,16,2816]{2,1,0:T(8,128)(2,1)S(1)}, u32[]{:S(2)}, u32[]{:S(2)}) %all-to-all-start) | async-done | bytes 2883616 | tf_op jit(solution)/shard_map/all_to_all | solution.py:335
  87.1 0.0 copy-done.3
  87.1 0.0 copy-done.4
  87.1 16.3 %analysis.1 = bf16[512,768]{1,0:T(8,128)(2,1)S(1)} custom-call(s32[1,1]{1,0:T(1,128)} %bitcast.6.total_ref, bf16[512,2816]{1,0:T(8,128)(2,1)S(1)} %bitcast.7, f32[1,2048]{1,0:T(1,128)S(1)} %bitcast.10, f32[1,2048]{1,0:T(1,128)S(1)} %bitcast.11), custom_call_target="tpu_custom_call" | custom-call | tf_op jit(solution)/shard_map/analysis/pallas_call | solution.py:336
  103.4 22.7 %all_to_all.10.back_ref = bf16[32,16,768]{2,1,0:T(8,128)(2,1)S(1)} all-to-all(bf16[32,16,768]{2,1,0:T(8,128)(2,1)S(1)} %bitcast.8), channel_id=1, replica_groups=mesh['mem'=32,'ty'=2,'tx'=2] {'mem'}, dimensions={0} | all-to-all | bytes 1572864 | tf_op jit(solution)/shard_map/all_to_all | solution.py:350
  126.1 1.1 deliver.1
Async XLA Ops:
  0.0 1.4 %copy-start = (f32[16,3,32,256]{3,2,1,0:T(8,128)S(1)}, f32[16,3,32,256]{3,2,1,0:T(8,128)}, u32[]{:S(2)}) copy-start(f32[16,3,32,256]{3,2,1,0:T(8,128)} %x_ref.1) | copy-start | bytes 4718596
  1.4 0.8 copy-start.2
  2.2 14.9 %copy-start.1 = (s32[1,1,65536]{2,1,0:T(1,128)S(1)}, s32[1,1,65536]{2,1,0:T(1,128)}, u32[]{:S(2)}) copy-start(s32[1,1,65536]{2,1,0:T(1,128)} %param.8) | copy-start | bytes 786436
  2.6 6.9 %collective-permute-start = (f32[37,16,256]{2,1,0:T(8,128)S(1)}, f32[37,16,256]{2,1,0:T(8,128)S(1)}, u32[]{:S(2)}, u32[]{:S(2)}) collective-permute-start(f32[37,16,256]{2,1,0:T(8,128)S(1)} %get-tuple-element.14), channel_id=1, source_target_pairs={{0,2},{2,0},{1,3},{3,1},{4,6},{6,4},{5,7},{7,5},{8,10},{10,8},{9,1... | collective-permute-start | bytes 1818632 | tf_op jit(solution)/shard_map/ppermute | solution.py:308
  2.7 6.8 %collective-permute-start.1 = (f32[14,16,128]{2,1,0:T(8,128)S(1)}, f32[14,16,128]{2,1,0:T(8,128)S(1)}, u32[]{:S(2)}, u32[]{:S(2)}) collective-permute-start(f32[14,16,128]{2,1,0:T(8,128)S(1)} %get-tuple-element.15), channel_id=1, source_target_pairs={{0,1},{1,0},{2,3},{3,2},{4,5},{5,4},{6,7},{7,6},{8,9},{9,8},{10,11... | collective-permute-start | bytes 344072 | tf_op jit(solution)/shard_map/ppermute | solution.py:309
  4.8 4.7 %collective-permute-start.2 = (f32[7,16,128]{2,1,0:T(8,128)S(1)}, f32[7,16,128]{2,1,0:T(8,128)S(1)}, u32[]{:S(2)}, u32[]{:S(2)}) collective-permute-start(f32[7,16,128]{2,1,0:T(8,128)S(1)} %get-tuple-element.16), channel_id=1, source_target_pairs={{0,3},{1,2},{2,1},{3,0},{4,7},{5,6},{6,5},{7,4},{8,11},{9,10},{10,... | collective-permute-start | bytes 172040 | tf_op jit(solution)/shard_map/ppermute | solution.py:310
  37.6 49.5 %copy-start.3 = (f32[1,1,2048]{2,1,0:T(1,128)S(1)}, f32[1,1,2048]{2,1,0:T(1,128)}, u32[]{:S(2)}) copy-start(f32[1,1,2048]{2,1,0:T(1,128)} %param.9) | copy-start | bytes 24580
  37.6 49.5 %copy-start.4 = (f32[1,1,2048]{2,1,0:T(1,128)S(1)}, f32[1,1,2048]{2,1,0:T(1,128)}, u32[]{:S(2)}) copy-start(f32[1,1,2048]{2,1,0:T(1,128)} %param.10) | copy-start | bytes 24580
  37.7 49.4 %all-to-all-start = ((bf16[32,16,2816]{2,1,0:T(8,128)(2,1)}), bf16[32,16,2816]{2,1,0:T(8,128)(2,1)S(1)}, u32[]{:S(2)}, u32[]{:S(2)}) async-start(bf16[32,16,2816]{2,1,0:T(8,128)(2,1)} %sample.1), calls=%async_computation | async-start | bytes 5767168 | tf_op jit(solution)/shard_map/all_to_all | solution.py:335

commit v3 on v2

--- a/solution.py
+++ b/solution.py
@@ -4,6 +4,7 @@
 from jax.experimental import pallas as pl
 from jax.experimental.pallas import tpu as pltpu
 from jax.sharding import PartitionSpec as P
+
 
 NSI = 12
 STEPS = 2
@@ -18,7 +19,9 @@
 HALO = 6
 WIDE_ROWS = CY + 2 * HALO
 WIDE_COLS = CX + 128
-PACK = 16
+EDGE = 2 * HALO
+COL_SLABS = 10
+CORNER_SLABS = 4
 CHUNK = 512
 PRODUCT = 1536
 BY_LANES = (2, 1, 1)
@@ -34,44 +37,58 @@
 
 
 def pack_edges(edges, per):
-    rows = edges.shape[0]
-    total = None
-    for place in range(rows // per):
-        part = pltpu.roll(edges[place * per : (place + 1) * per], HALO + PACK * place, 2)
-        if total is None:
-            total = part
-        else:
-            lane = lax.broadcasted_iota(jnp.int32, part.shape, 2)
-            total = jnp.where(lane >= PACK * place, part, total)
+    count = edges.shape[0]
+    total = pltpu.roll(edges[:per], HALO, 2)
+    for place in range(1, pl.cdiv(count, per)):
+        part = edges[place * per : min((place + 1) * per, count)]
+        size = part.shape[0]
+        lane = lax.broadcasted_iota(jnp.int32, part.shape, 2)
+        mixed = jnp.where(lane >= EDGE * place, pltpu.roll(part, HALO + EDGE * place, 2), total[:size])
+        total = mixed if size == per else jnp.concatenate([mixed, total[size:]], axis=0)
     return total
 
 
-def outgoing_kernel(x_ref, depth_in_ref, state_ref, depth_ref, rows_ref, cols_ref, corner_ref):
-    depth = depth_in_ref[...]
-    depth_ref[...] = depth
+def runs(count, per, size):
+    for place in range(pl.cdiv(count, per)):
+        at = place * per
+        end = min(at + per, count)
+        while at < end:
+            field, row = divmod(at, size)
+            length = min(end - at, size - row)
+            yield place, at - place * per, field, row, length
+            at += length
+
+
+def outgoing_kernel(x_ref, rate_ref, state_ref, rows_ref, cols_ref, corner_ref):
+    rate = rate_ref[...]
+    state_ref[FIELDS * CY] = rate[:16]
+    state_ref[FIELDS * CY + 1] = rate[16:]
     outer = (slice(0, HALO), slice(CY - HALO, CY))
+    edges, corners = [], []
     for field in range(FIELDS):
-        state_ref[field] = pltpu.einshape("mrc->rmc", x_ref[:, field])
-        block = state_ref[field]
-        edges = edge_lanes(block)
-        cols_ref[4 * field : 4 * field + 4] = pack_edges(edges, 4)
-        both = jnp.concatenate([edges[part] for part in outer], axis=0)
-        corner_ref[2 * field : 2 * field + 2] = pack_edges(both, 2)
+        block = pltpu.einshape("mrc->rmc", x_ref[:, field])
+        state_ref[field * CY : (field + 1) * CY] = block
+        edges.append(edge_lanes(block))
+        corners.extend(edges[field][part] for part in outer)
         rows_ref[12 * field : 12 * field + 6] = block[outer[0]]
         rows_ref[12 * field + 6 : 12 * field + 12] = block[outer[1]]
-    depth_edges = edge_lanes(depth)
-    cols_ref[12] = depth_edges[:16]
-    cols_ref[13] = depth_edges[16:]
-    rows_ref[36, 0:HALO] = depth[outer[0]]
-    rows_ref[36, HALO : 2 * HALO] = depth[outer[1]]
-    rows_ref[36, 2 * HALO : 16] = depth[0:4]
-    corner_ref[6, 0:HALO] = depth_edges[outer[0]]
-    corner_ref[6, HALO : 2 * HALO] = depth_edges[outer[1]]
-    corner_ref[6, 2 * HALO : 16] = depth_edges[0:4]
+    cols_ref[:COL_SLABS] = pack_edges(jnp.concatenate(edges, axis=0), COL_SLABS)
+    corner_ref[:CORNER_SLABS] = pack_edges(jnp.concatenate(corners, axis=0), CORNER_SLABS)
+    rate_edges = edge_lanes(rate)
+    lane = lax.broadcasted_iota(jnp.int32, (LOCAL, 128), 1)
+    cols_ref[COL_SLABS] = jnp.where(
+        lane < EDGE, pltpu.roll(rate_edges[:16], HALO, 1), pltpu.roll(rate_edges[16:], HALO + EDGE, 1)
+    )
+    rows_ref[36, 0:HALO] = rate[outer[0]]
+    rows_ref[36, HALO : 2 * HALO] = rate[outer[1]]
+    rows_ref[36, 2 * HALO : 16] = rate[0:4]
+    corner_ref[CORNER_SLABS, 0:HALO] = rate_edges[outer[0]]
+    corner_ref[CORNER_SLABS, HALO : 2 * HALO] = rate_edges[outer[1]]
+    corner_ref[CORNER_SLABS, 2 * HALO : 16] = rate_edges[0:4]
 
 
 def forecast_kernel(
-    state_ref, depth_ref, rows_ref, cols_ref, corner_ref, cells_ref, strips_ref, base_ref, one_ref, two_ref, rate_ref
+    state_ref, rows_ref, cols_ref, corner_ref, cells_ref, strips_ref, base_ref, one_ref, two_ref, rate_ref
 ):
     upper = slice(0, HALO)
     inner = slice(HALO, HALO + CY)
@@ -80,25 +97,27 @@
     rim = slice(CX, WIDE_COLS)
 
     for field in range(FIELDS):
-        base_ref[field, inner, :, main] = state_ref[field]
+        base_ref[field, inner, :, main] = state_ref[field * CY : (field + 1) * CY]
         base_ref[field, lower, :, main] = rows_ref[12 * field : 12 * field + 6]
         base_ref[field, upper, :, main] = rows_ref[12 * field + 6 : 12 * field + 12]
-        packed = cols_ref[4 * field : 4 * field + 4]
-        for place in range(8):
-            base_ref[field, HALO + 4 * place : HALO + 4 * place + 4, :, rim] = pltpu.roll(
-                packed, 128 - HALO - PACK * place, 2
-            )
-        packed = corner_ref[2 * field : 2 * field + 2]
-        for place in range(6):
-            start = HALO + CY + 2 * place if place < 3 else 2 * place - HALO
-            base_ref[field, start : start + 2, :, rim] = pltpu.roll(packed, (128 - HALO - PACK * place) % 128, 2)
-    rate_ref[inner, main] = -HALF_NU * depth_ref[...]
-    rate_ref[lower, main] = -HALF_NU * rows_ref[36, 0:HALO]
-    rate_ref[upper, main] = -HALF_NU * rows_ref[36, HALO : 2 * HALO]
-    rate_ref[HALO : HALO + 16, rim] = -HALF_NU * cols_ref[12]
-    rate_ref[HALO + 16 : HALO + 32, rim] = -HALF_NU * cols_ref[13]
-    rate_ref[lower, rim] = -HALF_NU * corner_ref[6, 0:HALO]
-    rate_ref[upper, rim] = -HALF_NU * corner_ref[6, HALO : 2 * HALO]
+    for place, slab, field, row, length in runs(FIELDS * CY, COL_SLABS, CY):
+        base_ref[field, HALO + row : HALO + row + length, :, rim] = pltpu.roll(
+            cols_ref[slab : slab + length], 128 - HALO - EDGE * place, 2
+        )
+    for place, slab, field, row, length in runs(FIELDS * 2 * HALO, CORNER_SLABS, 2 * HALO):
+        moved = pltpu.roll(corner_ref[slab : slab + length], 128 - HALO - EDGE * place, 2)
+        for step in range(length):
+            start = HALO + CY + row + step if row + step < HALO else row + step - HALO
+            base_ref[field, start, :, rim] = moved[step]
+    rate_ref[HALO : HALO + 16, main] = state_ref[FIELDS * CY]
+    rate_ref[HALO + 16 : HALO + 32, main] = state_ref[FIELDS * CY + 1]
+    rate_ref[lower, main] = rows_ref[36, 0:HALO]
+    rate_ref[upper, main] = rows_ref[36, HALO : 2 * HALO]
+    packed = cols_ref[COL_SLABS]
+    rate_ref[HALO : HALO + 16, rim] = pltpu.roll(packed, 128 - HALO, 1)
+    rate_ref[HALO + 16 : HALO + 32, rim] = pltpu.roll(packed, 128 - HALO - EDGE, 1)
+    rate_ref[lower, rim] = corner_ref[CORNER_SLABS, 0:HALO]
+    rate_ref[upper, rim] = corner_ref[CORNER_SLABS, HALO : 2 * HALO]
 
     def shift_zonal(row, carry):
         base_ref[1, row] = pltpu.roll(base_ref[1, row], 1, 1)
@@ -202,37 +221,45 @@
     return lax.dot_general(left, right, (dims, ((), ())), preferred_element_type=jnp.float32)
 
 
-def exact_product(matrix, column):
-    high = column.astype(jnp.bfloat16)
-    rest = column - high.astype(jnp.float32)
-    middle = rest.astype(jnp.bfloat16)
-    low = (rest - middle.astype(jnp.float32)).astype(jnp.bfloat16)
-    lane = lax.broadcasted_iota(jnp.int32, (MEMBERS, 128), 1)
-    wide = lambda part: jnp.broadcast_to(part.astype(jnp.float32), (MEMBERS, 128))
-    parts = jnp.where(lane == 0, wide(high), jnp.where(lane == 1, wide(middle), jnp.where(lane == 2, wide(low), 0.0)))
-    return jnp.sum(dot32(matrix, parts.astype(jnp.bfloat16)), axis=1, keepdims=True)
+def exact_product(row, matrix):
+    high = row.astype(jnp.bfloat16).astype(jnp.float32)
+    middle = (row - high).astype(jnp.bfloat16).astype(jnp.float32)
+    low = row - high - middle
+    line = lax.broadcasted_iota(jnp.int32, (LOCAL, MEMBERS), 0)
+    parts = jnp.where(line == 0, high, jnp.where(line == 1, middle, jnp.where(line == 2, low, 0.0)))
+    return jnp.sum(dot32(parts.astype(jnp.bfloat16), matrix), axis=0, keepdims=True)
 
 
 def analysis_kernel(
     total_ref, gathered_ref, values_ref, errors_ref, out_ref, dev_ref, root_ref, inverse_ref, correction_ref
 ):
-    total = total_ref[0, 0]
-    projected = jnp.zeros((MEMBERS, 8), jnp.float32)
-    for part in range(SLOTS // CHUNK):
-        span = slice(part * CHUNK, (part + 1) * CHUNK)
-        obs = gathered_ref[:, span].astype(jnp.float32)
-        mean = jnp.sum(obs, axis=0, keepdims=True) * (1.0 / MEMBERS)
-        slot = lax.broadcasted_iota(jnp.int32, (1, CHUNK), 1) + part * CHUNK
-        scale = (slot < total).astype(jnp.float32) / errors_ref[:, span]
-        scaled = ((obs - mean) * scale).astype(jnp.bfloat16)
-        innovation = ((values_ref[:, span] - mean) * scale).astype(jnp.bfloat16)
-        dev_ref[:, span] = scaled
-        rows = jnp.broadcast_to(innovation.astype(jnp.float32), (8, CHUNK)).astype(jnp.bfloat16)
-        projected = projected + dot32(scaled, rows, ((1,), (1,)))
+    prior = slice(0, SLOTS)
+
+    def add_rows(block, partial):
+        rows = gathered_ref[pl.ds(block * LOCAL, LOCAL), prior].astype(jnp.float32)
+        return partial + (rows[:8] + rows[8:])
+
+    blocks = MEMBERS // LOCAL
+    partial = lax.fori_loop(0, blocks, add_rows, jnp.zeros((8, SLOTS), jnp.float32), unroll=2)
+    mean = jnp.sum(partial, axis=0, keepdims=True) * (1.0 / MEMBERS)
+    slot = lax.broadcasted_iota(jnp.int32, (1, SLOTS), 1)
+    scale = (slot < total_ref[0, 0]).astype(jnp.float32) / errors_ref[...]
+    innovation = (values_ref[...] - mean) * scale
+    dev_ref[MEMBERS:, :] = jnp.broadcast_to(innovation, (LOCAL, SLOTS)).astype(jnp.bfloat16)
+
+    def center_rows(block, carry):
+        span = pl.ds(block * LOCAL, LOCAL)
+        rows = gathered_ref[span, prior].astype(jnp.float32)
+        dev_ref[span, :] = ((rows - mean) * scale).astype(jnp.bfloat16)
+        return carry
+
+    lax.fori_loop(0, blocks, center_rows, 0, unroll=2)
+    products = dot32(dev_ref[...], dev_ref[:MEMBERS, :], ((1,), (1,)))
+    projected = products[MEMBERS : MEMBERS + 1]
     diagonal = lax.broadcasted_iota(jnp.int32, (MEMBERS, MEMBERS), 0) == lax.broadcasted_iota(
         jnp.int32, (MEMBERS, MEMBERS), 1
     )
-    system = dot32(dev_ref[...], dev_ref[...], ((1,), (1,))) + jnp.where(diagonal, MEMBERS - 1.0, 0.0)
+    system = products[:MEMBERS] + jnp.where(diagonal, MEMBERS - 1.0, 0.0)
     frob = jnp.sqrt(jnp.sum(system * system, keepdims=True))
     root = (system / frob).astype(jnp.bfloat16)
     root_ref[...] = root
@@ -245,23 +272,27 @@
     root_ref[...] = dot32(root_ref[...], correction).astype(jnp.bfloat16)
 
     def iterate(index, carry):
-        correction_ref[...] = corrected(dot32(inverse_ref[...], root_ref[...]))
-        root_ref[...] = dot32(root_ref[...], correction_ref[...]).astype(jnp.bfloat16)
-        inverse_ref[...] = dot32(correction_ref[...], inverse_ref[...]).astype(jnp.bfloat16)
+        correction = corrected(dot32(inverse_ref[...], root_ref[...]))
+        correction_ref[...] = correction
+        new_inverse = dot32(correction_ref[...], inverse_ref[...]).astype(jnp.bfloat16)
+        root_ref[...] = dot32(root_ref[...], correction).astype(jnp.bfloat16)
+        inverse_ref[...] = new_inverse
         return carry
 
-    lax.fori_loop(0, NSI - 2, iterate, 0)
+    lax.fori_loop(0, NSI - 2, iterate, 0, unroll=10)
     correction_ref[...] = corrected(dot32(inverse_ref[...], root_ref[...]))
-    inverse = dot32(correction_ref[...], inverse_ref[...]).astype(jnp.bfloat16)
-    inner = exact_product(inverse, projected[:, 0:1])
-    mean_weights = exact_product(inverse, inner) / frob
-    root_ref[...] = (jnp.sqrt((MEMBERS - 1.0) / frob) * inverse.astype(jnp.float32) + mean_weights).astype(jnp.bfloat16)
+    root_ref[...] = dot32(correction_ref[...], inverse_ref[...]).astype(jnp.bfloat16).T
+    inner = exact_product(projected, root_ref[...])
+    mean_weights = exact_product(inner, root_ref[...]) / frob
+    inverse_ref[...] = (
+        jnp.sqrt((MEMBERS - 1.0) / frob) * root_ref[...].astype(jnp.float32) + mean_weights
+    ).astype(jnp.bfloat16)
     for part in range(FIELDS):
         span = slice(part * CX, (part + 1) * CX)
         strips = gathered_ref[:, SLOTS + part * CX : SLOTS + (part + 1) * CX].astype(jnp.float32)
         field_mean = jnp.sum(strips, axis=0, keepdims=True) * (1.0 / MEMBERS)
         deviation = (strips - field_mean).astype(jnp.bfloat16)
-        mixed = dot32(root_ref[...], deviation, ((0,), (0,)))
+        mixed = dot32(inverse_ref[...], deviation)
         out_ref[:, span] = (field_mean + mixed).astype(jnp.bfloat16)
 
 
@@ -280,6 +311,10 @@
 
 def params(mebibytes):
     return pltpu.CompilerParams(vmem_limit_bytes=mebibytes << 20)
+
+
+def hop(value, pairs, axis):
+    return lax.ppermute(value, axis, pairs)
 
 
 def shards(
@@ -291,33 +326,32 @@
     gauge_tally,
 ):
     f32, bf16 = jnp.float32, jnp.bfloat16
-    state, depth, rows, cols, corner = pl.pallas_call(
+    state, rows, cols, corner = pl.pallas_call(
         outgoing_kernel,
         out_shape=(
-            shape((FIELDS, CY, LOCAL, CX), f32),
-            shape((CY, CX), f32),
+            shape((FIELDS * CY + 2, LOCAL, CX), f32),
             shape((37, LOCAL, CX), f32),
-            shape((14, LOCAL, 128), f32),
-            shape((7, LOCAL, 128), f32),
+            shape((COL_SLABS + 1, LOCAL, 128), f32),
+            shape((CORNER_SLABS + 1, LOCAL, 128), f32),
         ),
         in_specs=[VMEM, VMEM],
-        out_specs=(VMEM,) * 5,
+        out_specs=(VMEM,) * 4,
         compiler_params=params(12),
         name="outgoing",
-    )(predicted_states, undisturbed_thickness_ratio)
-    rows = lax.ppermute(rows, "ty", [(0, 1), (1, 0)])
-    cols = lax.ppermute(cols, "tx", [(0, 1), (1, 0)])
-    corner = lax.ppermute(corner, ("ty", "tx"), [(0, 3), (1, 2), (2, 1), (3, 0)])
+    )(predicted_states, -HALF_NU * undisturbed_thickness_ratio)
+    cols = hop(cols, [(0, 1), (1, 0)], "tx")
+    corner = hop(corner, [(0, 3), (1, 2), (2, 1), (3, 0)], ("ty", "tx"))
+    rows = hop(rows, [(0, 1), (1, 0)], "ty")
     wide = (FIELDS, WIDE_ROWS, LOCAL, WIDE_COLS)
     cells, strips = pl.pallas_call(
         forecast_kernel,
         out_shape=(shape((CY // 2, LOCAL, 2 * CX), bf16), shape((CY, LOCAL, FIELDS * CX), bf16)),
-        in_specs=[VMEM] * 5,
+        in_specs=[VMEM] * 4,
         out_specs=(VMEM, VMEM),
         scratch_shapes=[pltpu.VMEM(wide, f32)] * 3 + [pltpu.VMEM((WIDE_ROWS + 4, WIDE_COLS), f32)],
         compiler_params=params(20),
         name="forecast",
-    )(state, depth, rows, cols, corner)
+    )(state, rows, cols, corner)
     taken = pl.pallas_call(
         sample_kernel,
         grid=(GROUP,),
@@ -338,7 +372,7 @@
         out_shape=shape((MEMBERS, FIELDS * CX), bf16),
         in_specs=[SMEM, VMEM, VMEM, VMEM],
         out_specs=VMEM,
-        scratch_shapes=[pltpu.VMEM((MEMBERS, SLOTS), bf16)] + [pltpu.VMEM((MEMBERS, MEMBERS), bf16)] * 3,
+        scratch_shapes=[pltpu.VMEM((MEMBERS + LOCAL, SLOTS), bf16)] + [pltpu.VMEM((MEMBERS, MEMBERS), bf16)] * 3,
         compiler_params=params(24),
         name="analysis",
     )(

time: 128 us -> 124 us (0.969)
  Pallas kernels: 45.9 us -> 43.5 us
  waiting for transfers between devices: 43.1 us -> 41.4 us
    pallas_call x1, Pallas kernels: 16.3 us -> 13.9 us  [shards(): pl.pallas_call(analysis_kernel, out_shape=shape((MEMBERS, FIELDS * CX), b...]
where the time goes in v3:
time: 124 us
  Pallas kernels  43.5 us (35%)
  waiting for transfers between devices  41.4 us (33%)
  blocking collectives  23 us (19%)
  starting transfers between devices  12.9 us (10%)
  local copies, waits for them, and re-layouts  1.42 us (1%)
    all_to_all x1, waiting for transfers between devices, shards(): lax.all_to_all(taken, 'mem', 0, 0, tiled=True).reshape(MEMBERS, BUNDLE)  37.5 us
    all_to_all x1, blocking collectives, shards(): lax.all_to_all(updated.reshape(GROUP, LOCAL, FIELDS * CX), 'mem', 0, 0, t...  23 us
    pallas_call x1, Pallas kernels, shards(): pl.pallas_call(sample_kernel, grid=(GROUP,), out_shape=shape((GROUP, LOCA...  20.5 us
    pallas_call x1, Pallas kernels, shards(): pl.pallas_call(analysis_kernel, out_shape=shape((MEMBERS, FIELDS * CX), b...  13.9 us
    all_to_all x1, starting transfers between devices, shards(): lax.all_to_all(taken, 'mem', 0, 0, tiled=True).reshape(MEMBERS, BUNDLE)  10.6 us
    pallas_call x1, Pallas kernels, shards(): pl.pallas_call(forecast_kernel, out_shape=(shape((CY // 2, LOCAL, 2 * CX)...  7.58 us
    ppermute x3, waiting for transfers between devices, hop(): return lax.ppermute(value, axis, pairs)  3.84 us
  transfers between devices with their start and end apart: 4, of which 2 were waited for; matrix products, arithmetic and copies ran while one was open for 0% of the time, Pallas kernels for 0%

profile of v3, /device:TPU:0, one launch (start us, length us, event | category | flops | bytes accessed | tf_op | source)
XLA Modules:
  0.0 123.6 jit_solution(474714889266088124)
XLA Ops:
  0.0 0.8 broadcast_multiply_fusion.rate_ref
  0.8 0.0 copy-start
  0.8 1.4 %copy-done = f32[16,3,32,256]{3,2,1,0:T(8,128)S(1)} copy-done((f32[16,3,32,256]{3,2,1,0:T(8,128)S(1)}, f32[16,3,32,256]{3,2,1,0:T(8,128)}, u32[]{:S(2)}) %copy-start) | copy-done | bytes 1572888
  2.2 0.0 copy-start.1
  2.2 0.4 outgoing.1
  2.6 0.1 collective-permute-start
  2.7 2.1 %collective-permute-start.1 = (f32[11,16,128]{2,1,0:T(8,128)S(1)}, f32[11,16,128]{2,1,0:T(8,128)S(1)}, u32[]{:S(2)}, u32[]{:S(2)}) collective-permute-start(f32[11,16,128]{2,1,0:T(8,128)S(1)} %get-tuple-element.13), channel_id=1, source_target_pairs={{0,1},{1,0},{2,3},{3,2},{4,5},{5,4},{6,7},{7,6},{8,9},{9,8},{10,11... | collective-permute-start | bytes 270344 | tf_op jit(solution)/shard_map/ppermute | solution.py:317
  4.8 0.0 collective-permute-start.2
  4.8 3.8 %collective-permute-done.2.corner_ref = f32[5,16,128]{2,1,0:T(8,128)S(1)} collective-permute-done((f32[5,16,128]{2,1,0:T(8,128)S(1)}, f32[5,16,128]{2,1,0:T(8,128)S(1)}, u32[]{:S(2)}, u32[]{:S(2)}) %collective-permute-start.2) | collective-permute-done | bytes 40992 | tf_op jit(solution)/shard_map/ppermute | solution.py:317
  8.7 0.0 collective-permute-done.1.cols_ref
  8.7 0.0 collective-permute-done.rows_ref
  8.7 7.6 %forecast.1 = (bf16[16,16,512]{2,1,0:T(8,128)(2,1)S(1)}, bf16[32,16,768]{2,1,0:T(8,128)(2,1)S(1)}) custom-call(f32[98,16,256]{2,1,0:T(8,128)S(1)} %get-tuple-element.11.state_ref, f32[37,16,256]{2,1,0:T(8,128)S(1)} %collective-permute-done.rows_ref, f32[11,16,128]{2,1,0:T(8,128)S(1)} %collective-permute-done.1.cols_ref, ...), custom_call_target="tpu_custom_call" | custom-call | tf_op jit(solution)/shard_map/forecast/pallas_call | solution.py:346
  16.3 0.0 copy-done.1
  16.3 20.5 %sample.1 = bf16[32,16,2816]{2,1,0:T(8,128)(2,1)} custom-call(bf16[16,16,512]{2,1,0:T(8,128)(2,1)S(1)} %get-tuple-element.15.cells_ref, bf16[32,16,768]{2,1,0:T(8,128)(2,1)S(1)} %get-tuple-element.16.strips_ref, s32[1,65536]{1,0:T(1,128)S(1)} %bitcast.9), custom_call_target="tpu_custom_call" | custom-call | tf_op jit(solution)/shard_map/sample/pallas_call | solution.py:355
  36.8 0.0 copy-start.2
  36.8 0.0 copy-start.3
  36.8 10.6 %all-to-all-start = ((bf16[32,16,2816]{2,1,0:T(8,128)(2,1)}), bf16[32,16,2816]{2,1,0:T(8,128)(2,1)S(1)}, u32[]{:S(2)}, u32[]{:S(2)}) async-start(bf16[32,16,2816]{2,1,0:T(8,128)(2,1)} %sample.1), calls=%async_computation | async-start | bytes 5767168 | tf_op jit(solution)/shard_map/all_to_all | solution.py:369
  48.1 37.5 %all-to-all-done = bf16[32,16,2816]{2,1,0:T(8,128)(2,1)S(1)} async-done(((bf16[32,16,2816]{2,1,0:T(8,128)(2,1)}), bf16[32,16,2816]{2,1,0:T(8,128)(2,1)S(1)}, u32[]{:S(2)}, u32[]{:S(2)}) %all-to-all-start) | async-done | bytes 2883616 | tf_op jit(solution)/shard_map/all_to_all | solution.py:369
  85.7 0.0 copy-done.2
  85.7 0.0 copy-done.3
  85.7 13.9 %analysis.1 = bf16[512,768]{1,0:T(8,128)(2,1)S(1)} custom-call(s32[1,1]{1,0:T(1,128)} %bitcast.6.total_ref, bf16[512,2816]{1,0:T(8,128)(2,1)S(1)} %bitcast.7, f32[1,2048]{1,0:T(1,128)S(1)} %bitcast.10, f32[1,2048]{1,0:T(1,128)S(1)} %bitcast.11), custom_call_target="tpu_custom_call" | custom-call | tf_op jit(solution)/shard_map/analysis/pallas_call | solution.py:370
  99.6 23.0 %all_to_all.10.back_ref = bf16[32,16,768]{2,1,0:T(8,128)(2,1)S(1)} all-to-all(bf16[32,16,768]{2,1,0:T(8,128)(2,1)S(1)} %bitcast.8), channel_id=1, replica_groups=mesh['mem'=32,'ty'=2,'tx'=2] {'mem'}, dimensions={0} | all-to-all | bytes 1572864 | tf_op jit(solution)/shard_map/all_to_all | solution.py:384
  122.6 1.1 deliver.1
Async XLA Ops:
  0.8 1.4 %copy-start = (f32[16,3,32,256]{3,2,1,0:T(8,128)S(1)}, f32[16,3,32,256]{3,2,1,0:T(8,128)}, u32[]{:S(2)}) copy-start(f32[16,3,32,256]{3,2,1,0:T(8,128)} %x_ref.1) | copy-start | bytes 4718596
  2.2 14.1 %copy-start.1 = (s32[1,1,65536]{2,1,0:T(1,128)S(1)}, s32[1,1,65536]{2,1,0:T(1,128)}, u32[]{:S(2)}) copy-start(s32[1,1,65536]{2,1,0:T(1,128)} %param.8) | copy-start | bytes 786436
  2.6 6.1 %collective-permute-start = (f32[37,16,256]{2,1,0:T(8,128)S(1)}, f32[37,16,256]{2,1,0:T(8,128)S(1)}, u32[]{:S(2)}, u32[]{:S(2)}) collective-permute-start(f32[37,16,256]{2,1,0:T(8,128)S(1)} %get-tuple-element.12), channel_id=1, source_target_pairs={{0,2},{2,0},{1,3},{3,1},{4,6},{6,4},{5,7},{7,5},{8,10},{10,8},{9,1... | collective-permute-start | bytes 1818632 | tf_op jit(solution)/shard_map/ppermute | solution.py:317
  2.7 6.0 %collective-permute-start.1 = (f32[11,16,128]{2,1,0:T(8,128)S(1)}, f32[11,16,128]{2,1,0:T(8,128)S(1)}, u32[]{:S(2)}, u32[]{:S(2)}) collective-permute-start(f32[11,16,128]{2,1,0:T(8,128)S(1)} %get-tuple-element.13), channel_id=1, source_target_pairs={{0,1},{1,0},{2,3},{3,2},{4,5},{5,4},{6,7},{7,6},{8,9},{9,8},{10,11... | collective-permute-start | bytes 270344 | tf_op jit(solution)/shard_map/ppermute | solution.py:317
  4.8 3.9 %collective-permute-start.2 = (f32[5,16,128]{2,1,0:T(8,128)S(1)}, f32[5,16,128]{2,1,0:T(8,128)S(1)}, u32[]{:S(2)}, u32[]{:S(2)}) collective-permute-start(f32[5,16,128]{2,1,0:T(8,128)S(1)} %get-tuple-element.14), channel_id=1, source_target_pairs={{0,3},{1,2},{2,1},{3,0},{4,7},{5,6},{6,5},{7,4},{8,11},{9,10},{10,... | collective-permute-start | bytes 122888 | tf_op jit(solution)/shard_map/ppermute | solution.py:317
  36.8 48.8 %copy-start.2 = (f32[1,1,2048]{2,1,0:T(1,128)S(1)}, f32[1,1,2048]{2,1,0:T(1,128)}, u32[]{:S(2)}) copy-start(f32[1,1,2048]{2,1,0:T(1,128)} %param.9) | copy-start | bytes 24580
  36.8 48.8 %copy-start.3 = (f32[1,1,2048]{2,1,0:T(1,128)S(1)}, f32[1,1,2048]{2,1,0:T(1,128)}, u32[]{:S(2)}) copy-start(f32[1,1,2048]{2,1,0:T(1,128)} %param.10) | copy-start | bytes 24580
  36.8 48.8 %all-to-all-start = ((bf16[32,16,2816]{2,1,0:T(8,128)(2,1)}), bf16[32,16,2816]{2,1,0:T(8,128)(2,1)S(1)}, u32[]{:S(2)}, u32[]{:S(2)}) async-start(bf16[32,16,2816]{2,1,0:T(8,128)(2,1)} %sample.1), calls=%async_computation | async-start | bytes 5767168 | tf_op jit(solution)/shard_map/all_to_all | solution.py:369

commit v4 on v3

--- a/solution.py
+++ b/solution.py
@@ -22,9 +22,10 @@
 EDGE = 2 * HALO
 COL_SLABS = 10
 CORNER_SLABS = 4
-CHUNK = 512
 PRODUCT = 1536
-BY_LANES = (2, 1, 1)
+SAMPLE_STEPS = ((512, 2), (512, 1), (512, 1))
+REGIONS = 2
+PARTS = 2
 
 HALF_NU = 0.35
 ONE_THIRD = 1.0 / 3.0
@@ -171,8 +172,6 @@
 
 
 def sample_kernel(cells_ref, strips_ref, place_ref, out_ref, halves_ref):
-    out_ref[0, :, SLOTS:] = strips_ref[0]
-
     @pl.when(pl.program_id(0) == 0)
     def _():
         def widen(pair, carry):
@@ -182,11 +181,11 @@
 
         lax.fori_loop(0, 16, widen, 0)
 
+    out_ref[:, :, SLOTS:] = strips_ref[...]
     cells = cells_ref[...].reshape(16 * LOCAL, 2 * CX)
 
-    def by_product(start, width):
-        span = slice(start, start + width)
-        place = place_ref[:, span]
+    def by_product(region, start, width):
+        place = place_ref[:, region * SLOTS + start : region * SLOTS + start + width]
         within = place & (2 * CX - 1)
         pair = place >> 9
         hit = lax.broadcasted_iota(jnp.int16, (2 * CX, width), 0) == within.astype(jnp.int16)
@@ -195,11 +194,10 @@
         taken = product[:LOCAL]
         for number in range(1, 16):
             taken = jnp.where(pair == number, product[number * LOCAL : (number + 1) * LOCAL], taken)
-        out_ref[0, :, span] = taken.astype(jnp.bfloat16)
-
-    def by_lanes(start):
-        span = slice(start, start + 128)
-        place = place_ref[:, span]
+        out_ref[region, :, start : start + width] = taken.astype(jnp.bfloat16)
+
+    def by_lanes(region, start):
+        place = place_ref[:, region * SLOTS + start : region * SLOTS + start + 128]
         lane = jnp.broadcast_to(place & 127, (8, 128))
         block = jnp.broadcast_to(place >> 7, (8, 128))
         taken = [jnp.zeros((8, 128), jnp.float32)] * 2
@@ -209,12 +207,16 @@
                 source = halves_ref[number, 8 * half : 8 * half + 8, :]
                 moved = jnp.take_along_axis(source, lane, axis=1, mode="promise_in_bounds")
                 taken[half] = jnp.where(match, moved, taken[half])
-        out_ref[0, :, span] = jnp.concatenate(taken, axis=0).astype(jnp.bfloat16)
-
-    for part in range(PRODUCT // CHUNK):
-        by_product(part * CHUNK, CHUNK)
-        for piece in range(BY_LANES[part]):
-            by_lanes(PRODUCT + 128 * (sum(BY_LANES[:part]) + piece))
+        out_ref[region, :, start : start + 128] = jnp.concatenate(taken, axis=0).astype(jnp.bfloat16)
+
+    for region in range(REGIONS):
+        start, rest = 0, PRODUCT
+        for width, count in SAMPLE_STEPS:
+            by_product(region, start, width)
+            start += width
+            for _ in range(count):
+                by_lanes(region, rest)
+                rest += 128
 
 
 def dot32(left, right, dims=((1,), (0,))):
@@ -233,28 +235,27 @@
 def analysis_kernel(
     total_ref, gathered_ref, values_ref, errors_ref, out_ref, dev_ref, root_ref, inverse_ref, correction_ref
 ):
-    prior = slice(0, SLOTS)
-
-    def add_rows(block, partial):
-        rows = gathered_ref[pl.ds(block * LOCAL, LOCAL), prior].astype(jnp.float32)
-        return partial + (rows[:8] + rows[8:])
-
+    slot = lax.broadcasted_iota(jnp.int32, (1, SLOTS), 1)
+    every = (slot < total_ref[0, 0]).astype(jnp.float32) / errors_ref[...]
+    products = None
     blocks = MEMBERS // LOCAL
-    partial = lax.fori_loop(0, blocks, add_rows, jnp.zeros((8, SLOTS), jnp.float32), unroll=2)
-    mean = jnp.sum(partial, axis=0, keepdims=True) * (1.0 / MEMBERS)
-    slot = lax.broadcasted_iota(jnp.int32, (1, SLOTS), 1)
-    scale = (slot < total_ref[0, 0]).astype(jnp.float32) / errors_ref[...]
-    innovation = (values_ref[...] - mean) * scale
-    dev_ref[MEMBERS:, :] = jnp.broadcast_to(innovation, (LOCAL, SLOTS)).astype(jnp.bfloat16)
-
-    def center_rows(block, carry):
-        span = pl.ds(block * LOCAL, LOCAL)
-        rows = gathered_ref[span, prior].astype(jnp.float32)
-        dev_ref[span, :] = ((rows - mean) * scale).astype(jnp.bfloat16)
-        return carry
-
-    lax.fori_loop(0, blocks, center_rows, 0, unroll=2)
-    products = dot32(dev_ref[...], dev_ref[:MEMBERS, :], ((1,), (1,)))
+    width = SLOTS // PARTS
+    for part in range(PARTS):
+        span = slice(part * width, (part + 1) * width)
+        sums = [jnp.zeros((8, width), jnp.float32) for _ in range(2)]
+        for block in range(blocks):
+            rows = gathered_ref[block * LOCAL : (block + 1) * LOCAL, span].astype(jnp.float32)
+            sums = [sums[0] + rows[:8], sums[1] + rows[8:]]
+        mean = jnp.sum(sums[0] + sums[1], axis=0, keepdims=True) * (1.0 / MEMBERS)
+        scale = every[:, span]
+        innovation = (values_ref[:, span] - mean) * scale
+        dev_ref[MEMBERS:, span] = jnp.broadcast_to(innovation, (LOCAL, width)).astype(jnp.bfloat16)
+        for block in range(blocks):
+            lines = slice(block * LOCAL, (block + 1) * LOCAL)
+            rows = gathered_ref[lines, span].astype(jnp.float32)
+            dev_ref[lines, span] = ((rows - mean) * scale).astype(jnp.bfloat16)
+        product = dot32(dev_ref[:, span], dev_ref[:MEMBERS, span], ((1,), (1,)))
+        products = product if products is None else products + product
     projected = products[MEMBERS : MEMBERS + 1]
     diagonal = lax.broadcasted_iota(jnp.int32, (MEMBERS, MEMBERS), 0) == lax.broadcasted_iota(
         jnp.int32, (MEMBERS, MEMBERS), 1
@@ -354,14 +355,14 @@
     )(state, rows, cols, corner)
     taken = pl.pallas_call(
         sample_kernel,
-        grid=(GROUP,),
+        grid=(GROUP // REGIONS,),
         out_shape=shape((GROUP, LOCAL, BUNDLE), bf16),
         in_specs=[
             pl.BlockSpec((CY // 2, LOCAL, 2 * CX), lambda region: (0, 0, 0)),
-            pl.BlockSpec((1, LOCAL, FIELDS * CX), lambda region: (region, 0, 0)),
-            pl.BlockSpec((1, SLOTS), lambda region: (0, region)),
+            pl.BlockSpec((REGIONS, LOCAL, FIELDS * CX), lambda region: (region, 0, 0)),
+            pl.BlockSpec((1, REGIONS * SLOTS), lambda region: (0, region)),
         ],
-        out_specs=pl.BlockSpec((1, LOCAL, BUNDLE), lambda region: (region, 0, 0)),
+        out_specs=pl.BlockSpec((REGIONS, LOCAL, BUNDLE), lambda region: (region, 0, 0)),
         scratch_shapes=[pltpu.VMEM((64, LOCAL, 128), jnp.float32)],
         compiler_params=params(52),
         name="sample",

time: 124 us -> 121 us (0.976)
  Pallas kernels: 43.5 us -> 40.3 us
    pallas_call x1, Pallas kernels: 20.5 us -> 18.3 us  [shards(): pl.pallas_call(sample_kernel, grid=(GROUP // REGIONS,), out_shape=shape((...]
where the time goes in v4:
time: 121 us; the launch traced here: 120 us
  waiting for transfers between devices  41.4 us (34%)
  Pallas kernels  40.3 us (33%)
  blocking collectives  23 us (19%)
  starting transfers between devices  12.9 us (11%)
  local copies, waits for them, and re-layouts  1.42 us (1%)
    all_to_all x1, waiting for transfers between devices, shards(): lax.all_to_all(taken, 'mem', 0, 0, tiled=True).reshape(MEMBERS, BUNDLE)  37.6 us
    all_to_all x1, blocking collectives, shards(): lax.all_to_all(updated.reshape(GROUP, LOCAL, FIELDS * CX), 'mem', 0, 0, t...  23 us
    pallas_call x1, Pallas kernels, shards(): pl.pallas_call(sample_kernel, grid=(GROUP // REGIONS,), out_shape=shape((...  18.3 us
    pallas_call x1, Pallas kernels, shards(): pl.pallas_call(analysis_kernel, out_shape=shape((MEMBERS, FIELDS * CX), b...  12.9 us
    all_to_all x1, starting transfers between devices, shards(): lax.all_to_all(taken, 'mem', 0, 0, tiled=True).reshape(MEMBERS, BUNDLE)  10.6 us
    pallas_call x1, Pallas kernels, shards(): pl.pallas_call(forecast_kernel, out_shape=(shape((CY // 2, LOCAL, 2 * CX)...  7.58 us
    ppermute x3, waiting for transfers between devices, hop(): return lax.ppermute(value, axis, pairs)  3.84 us
  transfers between devices with their start and end apart: 4, of which 2 were waited for; matrix products, arithmetic and copies ran while one was open for 0% of the time, Pallas kernels for 0%

profile of v4, /device:TPU:0, one launch (start us, length us, event | category | flops | bytes accessed | tf_op | source)
XLA Modules:
  0.0 120.4 jit_solution(11687237225111011979)
XLA Ops:
  0.0 0.8 broadcast_multiply_fusion.rate_ref
  0.8 0.0 copy-start
  0.8 1.4 %copy-done = f32[16,3,32,256]{3,2,1,0:T(8,128)S(1)} copy-done((f32[16,3,32,256]{3,2,1,0:T(8,128)S(1)}, f32[16,3,32,256]{3,2,1,0:T(8,128)}, u32[]{:S(2)}) %copy-start) | copy-done | bytes 1572888
  2.2 0.0 copy-start.1
  2.2 0.4 outgoing.1
  2.6 0.1 collective-permute-start
  2.7 2.1 %collective-permute-start.1 = (f32[11,16,128]{2,1,0:T(8,128)S(1)}, f32[11,16,128]{2,1,0:T(8,128)S(1)}, u32[]{:S(2)}, u32[]{:S(2)}) collective-permute-start(f32[11,16,128]{2,1,0:T(8,128)S(1)} %get-tuple-element.13), channel_id=1, source_target_pairs={{0,1},{1,0},{2,3},{3,2},{4,5},{5,4},{6,7},{7,6},{8,9},{9,8},{10,11... | collective-permute-start | bytes 270344 | tf_op jit(solution)/shard_map/ppermute | solution.py:318
  4.8 0.0 collective-permute-start.2
  4.8 3.8 %collective-permute-done.2.corner_ref = f32[5,16,128]{2,1,0:T(8,128)S(1)} collective-permute-done((f32[5,16,128]{2,1,0:T(8,128)S(1)}, f32[5,16,128]{2,1,0:T(8,128)S(1)}, u32[]{:S(2)}, u32[]{:S(2)}) %collective-permute-start.2) | collective-permute-done | bytes 40992 | tf_op jit(solution)/shard_map/ppermute | solution.py:318
  8.7 0.0 collective-permute-done.1.cols_ref
  8.7 0.0 collective-permute-done.rows_ref
  8.7 7.6 %forecast.1 = (bf16[16,16,512]{2,1,0:T(8,128)(2,1)S(1)}, bf16[32,16,768]{2,1,0:T(8,128)(2,1)S(1)}) custom-call(f32[98,16,256]{2,1,0:T(8,128)S(1)} %get-tuple-element.11.state_ref, f32[37,16,256]{2,1,0:T(8,128)S(1)} %collective-permute-done.rows_ref, f32[11,16,128]{2,1,0:T(8,128)S(1)} %collective-permute-done.1.cols_ref, ...), custom_call_target="tpu_custom_call" | custom-call | tf_op jit(solution)/shard_map/forecast/pallas_call | solution.py:347
  16.3 0.0 copy-done.1
  16.3 18.3 %sample.1 = bf16[32,16,2816]{2,1,0:T(8,128)(2,1)} custom-call(bf16[16,16,512]{2,1,0:T(8,128)(2,1)S(1)} %get-tuple-element.15.cells_ref, bf16[32,16,768]{2,1,0:T(8,128)(2,1)S(1)} %get-tuple-element.16.strips_ref, s32[1,65536]{1,0:T(1,128)S(1)} %bitcast.9), custom_call_target="tpu_custom_call" | custom-call | tf_op jit(solution)/shard_map/sample/pallas_call | solution.py:356
  34.6 0.0 copy-start.2
  34.6 0.0 copy-start.3
  34.6 10.6 %all-to-all-start = ((bf16[32,16,2816]{2,1,0:T(8,128)(2,1)}), bf16[32,16,2816]{2,1,0:T(8,128)(2,1)S(1)}, u32[]{:S(2)}, u32[]{:S(2)}) async-start(bf16[32,16,2816]{2,1,0:T(8,128)(2,1)} %sample.1), calls=%async_computation | async-start | bytes 5767168 | tf_op jit(solution)/shard_map/all_to_all | solution.py:370
  45.9 37.6 %all-to-all-done = bf16[32,16,2816]{2,1,0:T(8,128)(2,1)S(1)} async-done(((bf16[32,16,2816]{2,1,0:T(8,128)(2,1)}), bf16[32,16,2816]{2,1,0:T(8,128)(2,1)S(1)}, u32[]{:S(2)}, u32[]{:S(2)}) %all-to-all-start) | async-done | bytes 2883616 | tf_op jit(solution)/shard_map/all_to_all | solution.py:370
  83.4 0.0 copy-done.2
  83.4 0.0 copy-done.3
  83.4 12.9 %analysis.1 = bf16[512,768]{1,0:T(8,128)(2,1)S(1)} custom-call(s32[1,1]{1,0:T(1,128)} %bitcast.6.total_ref, bf16[512,2816]{1,0:T(8,128)(2,1)S(1)} %bitcast.7, f32[1,2048]{1,0:T(1,128)S(1)} %bitcast.10, f32[1,2048]{1,0:T(1,128)S(1)} %bitcast.11), custom_call_target="tpu_custom_call" | custom-call | tf_op jit(solution)/shard_map/analysis/pallas_call | solution.py:371
  96.4 23.0 %all_to_all.10.back_ref = bf16[32,16,768]{2,1,0:T(8,128)(2,1)S(1)} all-to-all(bf16[32,16,768]{2,1,0:T(8,128)(2,1)S(1)} %bitcast.8), channel_id=1, replica_groups=mesh['mem'=32,'ty'=2,'tx'=2] {'mem'}, dimensions={0} | all-to-all | bytes 1572864 | tf_op jit(solution)/shard_map/all_to_all | solution.py:385
  119.3 1.1 deliver.1
Async XLA Ops:
  0.8 1.4 %copy-start = (f32[16,3,32,256]{3,2,1,0:T(8,128)S(1)}, f32[16,3,32,256]{3,2,1,0:T(8,128)}, u32[]{:S(2)}) copy-start(f32[16,3,32,256]{3,2,1,0:T(8,128)} %x_ref.1) | copy-start | bytes 4718596
  2.2 14.1 %copy-start.1 = (s32[1,1,65536]{2,1,0:T(1,128)S(1)}, s32[1,1,65536]{2,1,0:T(1,128)}, u32[]{:S(2)}) copy-start(s32[1,1,65536]{2,1,0:T(1,128)} %param.8) | copy-start | bytes 786436
  2.6 6.1 %collective-permute-start = (f32[37,16,256]{2,1,0:T(8,128)S(1)}, f32[37,16,256]{2,1,0:T(8,128)S(1)}, u32[]{:S(2)}, u32[]{:S(2)}) collective-permute-start(f32[37,16,256]{2,1,0:T(8,128)S(1)} %get-tuple-element.12), channel_id=1, source_target_pairs={{0,2},{2,0},{1,3},{3,1},{4,6},{6,4},{5,7},{7,5},{8,10},{10,8},{9,1... | collective-permute-start | bytes 1818632 | tf_op jit(solution)/shard_map/ppermute | solution.py:318
  2.7 6.0 %collective-permute-start.1 = (f32[11,16,128]{2,1,0:T(8,128)S(1)}, f32[11,16,128]{2,1,0:T(8,128)S(1)}, u32[]{:S(2)}, u32[]{:S(2)}) collective-permute-start(f32[11,16,128]{2,1,0:T(8,128)S(1)} %get-tuple-element.13), channel_id=1, source_target_pairs={{0,1},{1,0},{2,3},{3,2},{4,5},{5,4},{6,7},{7,6},{8,9},{9,8},{10,11... | collective-permute-start | bytes 270344 | tf_op jit(solution)/shard_map/ppermute | solution.py:318
  4.8 3.9 %collective-permute-start.2 = (f32[5,16,128]{2,1,0:T(8,128)S(1)}, f32[5,16,128]{2,1,0:T(8,128)S(1)}, u32[]{:S(2)}, u32[]{:S(2)}) collective-permute-start(f32[5,16,128]{2,1,0:T(8,128)S(1)} %get-tuple-element.14), channel_id=1, source_target_pairs={{0,3},{1,2},{2,1},{3,0},{4,7},{5,6},{6,5},{7,4},{8,11},{9,10},{10,... | collective-permute-start | bytes 122888 | tf_op jit(solution)/shard_map/ppermute | solution.py:318
  34.6 48.9 %copy-start.2 = (f32[1,1,2048]{2,1,0:T(1,128)S(1)}, f32[1,1,2048]{2,1,0:T(1,128)}, u32[]{:S(2)}) copy-start(f32[1,1,2048]{2,1,0:T(1,128)} %param.9) | copy-start | bytes 24580
  34.6 48.9 %copy-start.3 = (f32[1,1,2048]{2,1,0:T(1,128)S(1)}, f32[1,1,2048]{2,1,0:T(1,128)}, u32[]{:S(2)}) copy-start(f32[1,1,2048]{2,1,0:T(1,128)} %param.10) | copy-start | bytes 24580
  34.6 48.9 %all-to-all-start = ((bf16[32,16,2816]{2,1,0:T(8,128)(2,1)}), bf16[32,16,2816]{2,1,0:T(8,128)(2,1)S(1)}, u32[]{:S(2)}, u32[]{:S(2)}) async-start(bf16[32,16,2816]{2,1,0:T(8,128)(2,1)} %sample.1), calls=%async_computation | async-start | bytes 5767168 | tf_op jit(solution)/shard_map/all_to_all | solution.py:370
